TPU v7x, 1024 devices: a whole 4x4x32 slice. The times are simulated.
1024 devices in a mesh: gx: 4 (over y), gy: 8 (over z_hi, core), gz: 32 (over z_lo, x).
Axes of the slice: x: 4, y: 4, z: 32 (z_hi: 4, z_lo: 8; z = z_hi * 8 + z_lo), core: 2. Of those that a mesh axis runs over, the one named last changes fastest.
Arguments:
- offsets: float32 [4, 8, 32, 3, 128], P('gx', 'gy', 'gz'), may hold values from 0 to 10
- features: bfloat16 [4, 8, 32, 128, 256], P('gx', 'gy', 'gz'), may hold values from -6 to 6
- counts: int32 [4, 8, 32], P('gx', 'gy', 'gz'), may hold values from 64 to 128
- mask: int32 [4, 8, 32, 128], P('gx', 'gy', 'gz'), may hold values 0 or 1
- targets: float32 [4, 8, 32, 3, 128], P('gx', 'gy', 'gz'), may hold values from -6 to 6
- w_in: bfloat16 [256, 256], replicated, may hold values from -0.375 to 0.375
- radial: float32 [6, 256], replicated, may hold values from -5 to 5
- readout: float32 [256], replicated, may hold values from -0.375 to 0.375
Outputs:
- prediction: float32 [4, 8, 32, 3, 128], P('gx', 'gy', 'gz')
- grad_features: float32 [4, 8, 32, 128, 256], P('gx', 'gy', 'gz')
All inputs are finite; a program needn't handle non-finite values. No bound on the sum of `mask` on one device may be relied on, other than what follows from the above.
Results may differ from a plain program's by a relative error of at most 0.0065.
Values may be sent and summed in bfloat16 or wider, within the bound.
A program may use at most 64 MiB of HBM per device.

v0:
```python
import jax
import jax.numpy as jnp
from jax import lax
from jax.sharding import PartitionSpec as P

EDGE = 10.0
CUT = 5.0
GAMMA = 20.0
LOSS_WEIGHT = 16.0


def padded(shard, sides, width):
    for axis, dim in sides:
        size, length = (lax.axis_size(axis), shard.shape[dim])
        up = [(i, (i + 1) % size) for i in range(size)]
        down = [(j, i) for i, j in up]
        last = lax.slice_in_dim(shard, length - width, length, axis=dim)
        leading = lax.slice_in_dim(shard, 0, width, axis=dim)
        before = lax.ppermute(last, axis, up)
        after = lax.ppermute(leading, axis, down)
        shard = jnp.concatenate([before, shard, after], axis=dim)
    return shard


def slot_shift(first, count):
    slot = first + jnp.arange(count, dtype=jnp.int32)
    step_x = slot // 9 - 1
    step_y = slot // 3 % 3 - 1
    step_z = slot % 3 - 1
    return jnp.stack([step_x, step_y, step_z], 1).astype(jnp.float32) * EDGE


def build_kernels(own, near, first, count, bases):
    atoms = own.shape[1]
    shift = slot_shift(first, count)
    placed = near[:, :3, :] + shift[:, :, None]
    placed = jnp.transpose(placed, (1, 0, 2)).reshape(3, count * atoms)
    weight_near = near[:, 3, :].reshape(count * atoms)
    apart = placed[:, None, :] - own[:3, :, None]
    ratio = (apart[0] * apart[0] + apart[1] * apart[1] + apart[2] * apart[2]) / (CUT * CUT)
    column = first * atoms + jnp.arange(count * atoms, dtype=jnp.int32)
    same = column[None, :] == (13 * atoms + jnp.arange(atoms, dtype=jnp.int32))[:, None]
    envelope = jnp.where(same, 0.0, jnp.square(jnp.maximum(1.0 - ratio, 0.0)))
    envelope = envelope * own[3][:, None] * weight_near[None, :]
    centers = jnp.arange(bases).astype(jnp.float32) / (bases - 1)
    radial_part = envelope[None] * jnp.exp(
        -GAMMA * jnp.square(ratio[None] - centers[:, None, None])
    )
    direction_part = envelope[None] * apart / CUT
    return jnp.concatenate([radial_part, direction_part], 0).astype(jnp.bfloat16)


def on_device(offsets, features, counts, mask, targets, w_in, radial, readout):
    atoms = features.shape[3]
    width = features.shape[4]
    bases = radial.shape[0]
    hp = lax.Precision.HIGHEST
    occ = (jnp.arange(atoms, dtype=jnp.int32) < counts[0, 0, 0]).astype(jnp.float32)
    own = jnp.concatenate([offsets[0, 0, 0], occ[None, :]], 0)
    near = padded(own.reshape(1, 1, 1, 4, atoms), (("gx", 0), ("gy", 1), ("gz", 2)), 1)
    near = near.reshape(27, 4, atoms)
    proj = jnp.dot(features[0, 0, 0], w_in, preferred_element_type=jnp.float32).astype(jnp.bfloat16)
    near_proj = padded(proj.reshape(1, 1, 1, atoms, width), (("gx", 0), ("gy", 1), ("gz", 2)), 1)
    near_proj = near_proj.reshape(27 * atoms, width)

    def forward_plane(total, plane):
        first = plane * 9
        kern = build_kernels(own, lax.dynamic_slice_in_dim(near, first, 9, 0), first, 9, bases)
        block = lax.dynamic_slice_in_dim(near_proj, first * atoms, 9 * atoms, 0)
        total = total + jnp.einsum("kij,jf->kif", kern, block, preferred_element_type=jnp.float32)
        return (total, kern)

    start = jnp.zeros((bases + 3, atoms, width), jnp.float32)
    msg, kept = lax.scan(forward_plane, start, jnp.arange(3, dtype=jnp.int32))
    pre = jnp.einsum("bf,bif->if", radial, msg[:bases], precision=hp)
    gate = jax.nn.sigmoid(pre)
    gates = readout[None, :] * gate
    gates_bf = gates.astype(jnp.bfloat16)
    vec = msg[bases:]
    pred = jnp.einsum("cif,if->ci", vec, gates, precision=hp)
    err = (
        LOSS_WEIGHT
        * mask[0, 0, 0].astype(jnp.float32)[None, :]
        * occ[None, :]
        * (pred - targets[0, 0, 0])
    )
    slope = (
        jnp.einsum("ci,cif->if", err, vec, precision=hp) * readout[None, :] * gate * (1.0 - gate)
    )
    slope = slope.astype(jnp.bfloat16)
    near_err = padded(err.reshape(1, 1, 1, 3, atoms), (("gx", 0), ("gy", 1), ("gz", 2)), 1)
    near_err = jnp.transpose(near_err.reshape(27, 3, atoms), (1, 0, 2)).reshape(3, 27 * atoms)
    stacked = jnp.concatenate([slope, gates_bf], 1).reshape(1, 1, 1, atoms, 2 * width)
    both = padded(stacked, (("gx", 0), ("gy", 1), ("gz", 2)), 1)
    both = both.reshape(27 * atoms, 2 * width)
    near_slope = both[:, :width]
    near_gates = both[:, width:]

    def backward_plane(total, plane):
        first = plane * 9
        kern = kept[plane]
        err_block = lax.dynamic_slice_in_dim(near_err, first * atoms, 9 * atoms, 1)
        slope_block = lax.dynamic_slice_in_dim(near_slope, first * atoms, 9 * atoms, 0)
        gate_block = lax.dynamic_slice_in_dim(near_gates, first * atoms, 9 * atoms, 0)
        wide = kern[bases:].astype(jnp.float32)
        pairs = (
            wide[0] * err_block[0][None, :]
            + wide[1] * err_block[1][None, :]
            + wide[2] * err_block[2][None, :]
        )
        pairs = pairs.astype(jnp.bfloat16)
        radial_sum = jnp.einsum(
            "bij,jf->bif", kern[:bases], slope_block, preferred_element_type=jnp.float32
        )
        cross = jnp.dot(pairs, gate_block, preferred_element_type=jnp.float32)
        return ((total[0] + radial_sum, total[1] + cross), None)

    begin = (jnp.zeros((bases, atoms, width), jnp.float32), jnp.zeros((atoms, width), jnp.float32))
    sums, unused = lax.scan(backward_plane, begin, jnp.arange(3, dtype=jnp.int32))
    back = jnp.einsum("bf,bif->if", radial, sums[0], precision=hp) - sums[1]
    grad = lax.dot_general(
        back.astype(jnp.bfloat16),
        w_in,
        (((1,), (1,)), ((), ())),
        preferred_element_type=jnp.float32,
    )
    return (pred.reshape(1, 1, 1, 3, atoms), grad.reshape(1, 1, 1, atoms, width))


def solution(mesh):
    in_specs = (
        P("gx", "gy", "gz", None, None),
        P("gx", "gy", "gz", None, None),
        P("gx", "gy", "gz"),
        P("gx", "gy", "gz", None),
        P("gx", "gy", "gz", None, None),
        P(),
        P(),
        P(),
    )
    out_specs = (P("gx", "gy", "gz", None, None), P("gx", "gy", "gz", None, None))
    return jax.shard_map(
        on_device, mesh=mesh, in_specs=in_specs, out_specs=out_specs, check_vma=False
    )
```

profile of v0, /device:TPU:8, one launch (start us, length us, event | category | flops | bytes accessed | tf_op | source)
XLA Modules:
  0.0 293.9 jit_solution(3944486071107522972)
XLA Ops:
  2.5 15.0 %collective-permute-start.7 = (bf16[1,1,1,128,256]{4,3,2,1,0:T(8,128)(2,1)S(1)}, bf16[1,1,1,128,256]{4,3,2,1,0:T(8,128)(2,1)S(1)}, u32[]{:S(2)}, u32[]{:S(2)}) collective-permute-start(bf16[1,1,1,128,256]{4,3,2,1,0:T(8,128)(2,1)S(1)} %fusion.43), channel_id=1, source_target_pairs={{256,0},{512,256},{768,512},{0,768},{257,1},{513,257},{769,513},{1... | collective-permute-start | bytes 196616 | tf_op jit(solution)/shard_map/ppermute | solution.py:20
  19.5 4.2 %collective-permute-done.6 = bf16[1,1,1,128,256]{4,3,2,1,0:T(8,128)(2,1)S(1)} collective-permute-done((bf16[1,1,1,128,256]{4,3,2,1,0:T(8,128)(2,1)S(1)}, bf16[1,1,1,128,256]{4,3,2,1,0:T(8,128)(2,1)S(1)}, u32[]{:S(2)}, u32[]{:S(2)}) %collective-permute-start.6) | collective-permute-done | bytes 65568 | tf_op jit(solution)/shard_map/ppermute | solution.py:19
  23.7 9.6 %collective-permute-start.9 = (bf16[3,1,1,128,256]{4,3,2,1,0:T(8,128)(2,1)S(1)}, bf16[3,1,1,128,256]{4,3,2,1,0:T(8,128)(2,1)S(1)}, u32[]{:S(2)}, u32[]{:S(2)}) collective-permute-start(bf16[3,1,1,128,256]{4,3,2,1,0:T(8,128)(2,1)S(1)} %pad_maximum_fusion.5), channel_id=1, source_target_pairs={{32,0},{64,32},{96,64},{128,96},{160,128},{192,160},{224,192},{0,2... | collective-permute-start | bytes 589832 | tf_op jit(solution)/shard_map/ppermute | solution.py:20
  36.7 14.9 %collective-permute-done.9 = bf16[3,1,1,128,256]{4,3,2,1,0:T(8,128)(2,1)S(1)} collective-permute-done((bf16[3,1,1,128,256]{4,3,2,1,0:T(8,128)(2,1)S(1)}, bf16[3,1,1,128,256]{4,3,2,1,0:T(8,128)(2,1)S(1)}, u32[]{:S(2)}, u32[]{:S(2)}) %collective-permute-start.9) | collective-permute-done | bytes 196640 | tf_op jit(solution)/shard_map/ppermute | solution.py:20
  51.5 12.0 %collective-permute-done.8 = bf16[3,1,1,128,256]{4,3,2,1,0:T(8,128)(2,1)S(1)} collective-permute-done((bf16[3,1,1,128,256]{4,3,2,1,0:T(8,128)(2,1)S(1)}, bf16[3,1,1,128,256]{4,3,2,1,0:T(8,128)(2,1)S(1)}, u32[]{:S(2)}, u32[]{:S(2)}) %collective-permute-start.8) | collective-permute-done | bytes 196640 | tf_op jit(solution)/shard_map/ppermute | solution.py:19
  63.6 8.0 %collective-permute-start.11 = (bf16[3,3,1,128,256]{4,3,2,1,0:T(8,128)(2,1)S(1)}, bf16[3,3,1,128,256]{4,3,2,1,0:T(8,128)(2,1)S(1)}, u32[]{:S(2)}, u32[]{:S(2)}) collective-permute-start(bf16[3,3,1,128,256]{4,3,2,1,0:T(8,128)(2,1)S(1)} %pad_maximum_fusion.3), channel_id=1, source_target_pairs={{1,0},{2,1},{3,2},{4,3},{5,4},{6,5},{7,6},{8,7},{9,8},{10,9},{11,1... | collective-permute-start | bytes 1769480 | tf_op jit(solution)/shard_map/ppermute | solution.py:20
  73.5 4.9 %collective-permute-start.1 = (f32[1,1,1,4,128]{4,3,2,1,0:T(4,128)S(1)}, f32[1,1,1,4,128]{4,3,2,1,0:T(4,128)S(1)}, u32[]{:S(2)}, u32[]{:S(2)}) collective-permute-start(f32[1,1,1,4,128]{4,3,2,1,0:T(4,128)S(1)} %maximum_bitcast_fusion.1), channel_id=1, source_target_pairs={{256,0},{512,256},{768,512},{0,768},{257,1},{513,257},{769,513},{1... | collective-permute-start | bytes 6152 | tf_op jit(solution)/shard_map/ppermute | solution.py:20
  80.3 3.5 %collective-permute-done = f32[1,1,1,4,128]{4,3,2,1,0:T(4,128)S(1)} collective-permute-done((f32[1,1,1,4,128]{4,3,2,1,0:T(4,128)S(1)}, f32[1,1,1,4,128]{4,3,2,1,0:T(4,128)S(1)}, u32[]{:S(2)}, u32[]{:S(2)}) %collective-permute-start) | collective-permute-done | bytes 2080 | tf_op jit(solution)/shard_map/ppermute | solution.py:19
  88.2 11.2 %collective-permute-done.2 = f32[3,1,1,4,128]{4,3,2,1,0:T(4,128)S(1)} collective-permute-done((f32[3,1,1,4,128]{4,3,2,1,0:T(4,128)S(1)}, f32[3,1,1,4,128]{4,3,2,1,0:T(4,128)S(1)}, u32[]{:S(2)}, u32[]{:S(2)}) %collective-permute-start.2) | collective-permute-done | bytes 6176 | tf_op jit(solution)/shard_map/ppermute | solution.py:19
  99.4 12.6 %collective-permute-start.5 = (f32[3,3,1,4,128]{4,3,2,1,0:T(4,128)S(1)}, f32[3,3,1,4,128]{4,3,2,1,0:T(4,128)S(1)}, u32[]{:S(2)}, u32[]{:S(2)}) collective-permute-start(f32[3,3,1,4,128]{4,3,2,1,0:T(4,128)S(1)} %pad_maximum_fusion.8), channel_id=1, source_target_pairs={{1,0},{2,1},{3,2},{4,3},{5,4},{6,5},{7,6},{8,7},{9,8},{10,9},{11,1... | collective-permute-start | bytes 55304 | tf_op jit(solution)/shard_map/ppermute | solution.py:20
  114.1 12.4 %collective-permute-done.4 = f32[3,3,1,4,128]{4,3,2,1,0:T(4,128)S(1)} collective-permute-done((f32[3,3,1,4,128]{4,3,2,1,0:T(4,128)S(1)}, f32[3,3,1,4,128]{4,3,2,1,0:T(4,128)S(1)}, u32[]{:S(2)}, u32[]{:S(2)}) %collective-permute-start.4) | collective-permute-done | bytes 18464 | tf_op jit(solution)/shard_map/ppermute | solution.py:19
  127.9 37.7 %while.31 = (s32[]{:T(128)}, f32[9,128,256]{2,1,0:T(8,128)}, bf16[3,9,128,1152]{3,2,1,0:T(8,128)(2,1)}, s32[3]{0:T(128)S(1)}, f32[27,4,128]{2,1,0:T(4,128)S(1)},...) while((s32[]{:T(128)}, f32[9,128,256]{2,1,0:T(8,128)}, ...), condition=%wide.region_1.2_spmd.clone, body=%wide.region_0.1_spmd.clone.sunk | while | flops 695260416 | bytes 22856984 | solution.py:74
  134.5 3.9 %fusion.88 = f32[9,128,256]{2,1,0:T(8,128)} fusion(bf16[3,128,1152]{2,1,0:T(8,128)(2,1)} %get-tuple-element.478, bf16[6,128,1152]{2,1,0:T(8,128)(2,1)} %get-tuple-element.480, f32[9,128,256]{2,1,0:T(8,128)} %get-tuple-element.510, bf16[3456,256]{1,0:T(8,128)(2,1)} %get-tuple-element.530, s32[]{:T(128)S(6)} %select_n.143, pred[]{:T(512)S(6)} %compare.6), kind=kOutput, calls=%fused_computation.8.clone.1 | convolution fusion | flops 681394176 | bytes 5603333 | tf_op jit(solution)/shard_map/while/body/eval_jaxpr/kij,jf->kif/dot_general | solution.py:70
  146.8 4.3 %fusion.88 = f32[9,128,256]{2,1,0:T(8,128)} fusion(bf16[3,128,1152]{2,1,0:T(8,128)(2,1)} %get-tuple-element.478, bf16[6,128,1152]{2,1,0:T(8,128)(2,1)} %get-tuple-element.480, f32[9,128,256]{2,1,0:T(8,128)} %get-tuple-element.510, bf16[3456,256]{1,0:T(8,128)(2,1)} %get-tuple-element.530, s32[]{:T(128)S(6)} %select_n.143, pred[]{:T(512)S(6)} %compare.6), kind=kOutput, calls=%fused_computation.8.clone.1 | convolution fusion | flops 681394176 | bytes 5603333 | tf_op jit(solution)/shard_map/while/body/eval_jaxpr/kij,jf->kif/dot_general | solution.py:70
  159.5 4.3 %fusion.88 = f32[9,128,256]{2,1,0:T(8,128)} fusion(bf16[3,128,1152]{2,1,0:T(8,128)(2,1)} %get-tuple-element.478, bf16[6,128,1152]{2,1,0:T(8,128)(2,1)} %get-tuple-element.480, f32[9,128,256]{2,1,0:T(8,128)} %get-tuple-element.510, bf16[3456,256]{1,0:T(8,128)(2,1)} %get-tuple-element.530, s32[]{:T(128)S(6)} %select_n.143, pred[]{:T(512)S(6)} %compare.6), kind=kOutput, calls=%fused_computation.8.clone.1 | convolution fusion | flops 681394176 | bytes 5603333 | tf_op jit(solution)/shard_map/while/body/eval_jaxpr/kij,jf->kif/dot_general | solution.py:70
  177.6 3.1 %collective-permute-done.12 = bf16[1,1,1,128,512]{4,3,2,1,0:T(8,128)(2,1)S(1)} collective-permute-done((bf16[1,1,1,128,512]{4,3,2,1,0:T(8,128)(2,1)S(1)}, bf16[1,1,1,128,512]{4,3,2,1,0:T(8,128)(2,1)S(1)}, u32[]{:S(2)}, u32[]{:S(2)}) %collective-permute-start.12) | collective-permute-done | bytes 131104 | tf_op jit(solution)/shard_map/ppermute | solution.py:19
  185.1 9.5 %collective-permute-done.15 = bf16[3,1,1,128,512]{4,3,2,1,0:T(8,128)(2,1)S(1)} collective-permute-done((bf16[3,1,1,128,512]{4,3,2,1,0:T(8,128)(2,1)S(1)}, bf16[3,1,1,128,512]{4,3,2,1,0:T(8,128)(2,1)S(1)}, u32[]{:S(2)}, u32[]{:S(2)}) %collective-permute-start.15) | collective-permute-done | bytes 393248 | tf_op jit(solution)/shard_map/ppermute | solution.py:20
  194.6 13.6 %collective-permute-done.14 = bf16[3,1,1,128,512]{4,3,2,1,0:T(8,128)(2,1)S(1)} collective-permute-done((bf16[3,1,1,128,512]{4,3,2,1,0:T(8,128)(2,1)S(1)}, bf16[3,1,1,128,512]{4,3,2,1,0:T(8,128)(2,1)S(1)}, u32[]{:S(2)}, u32[]{:S(2)}) %collective-permute-start.14) | collective-permute-done | bytes 393248 | tf_op jit(solution)/shard_map/ppermute | solution.py:19
  211.5 3.9 %collective-permute-start.16 = (bf16[3,3,1,128,512]{4,3,2,1,0:T(8,128)(2,1)}, bf16[3,3,1,128,512]{4,3,2,1,0:T(8,128)(2,1)}, u32[]{:S(2)}, u32[]{:S(2)}) collective-permute-start(bf16[3,3,1,128,512]{4,3,2,1,0:T(8,128)(2,1)} %pad_maximum_fusion.2), channel_id=1, source_target_pairs={{0,1},{1,2},{2,3},{3,4},{4,5},{5,6},{6,7},{7,8},{8,9},{9,10},{10,1... | collective-permute-start | bytes 3538952 | tf_op jit(solution)/shard_map/ppermute | solution.py:19
  215.4 3.1 %collective-permute-start.19 = (f32[1,1,1,3,128]{4,3,2,1,0:T(4,128)S(1)}, f32[1,1,1,3,128]{4,3,2,1,0:T(4,128)S(1)}, u32[]{:S(2)}, u32[]{:S(2)}) collective-permute-start(f32[1,1,1,3,128]{4,3,2,1,0:T(4,128)S(1)} %get-tuple-element.370), channel_id=1, source_target_pairs={{256,0},{512,256},{768,512},{0,768},{257,1},{513,257},{769,513},{1... | collective-permute-start | bytes 4616 | tf_op jit(solution)/shard_map/ppermute | solution.py:20
  228.4 11.2 %collective-permute-done.20 = f32[3,1,1,3,128]{4,3,2,1,0:T(4,128)S(1)} collective-permute-done((f32[3,1,1,3,128]{4,3,2,1,0:T(4,128)S(1)}, f32[3,1,1,3,128]{4,3,2,1,0:T(4,128)S(1)}, u32[]{:S(2)}, u32[]{:S(2)}) %collective-permute-start.20) | collective-permute-done | bytes 4640 | tf_op jit(solution)/shard_map/ppermute | solution.py:19
  239.6 10.6 %collective-permute-start.23 = (f32[3,3,1,3,128]{4,3,2,1,0:T(4,128)S(1)}, f32[3,3,1,3,128]{4,3,2,1,0:T(4,128)S(1)}, u32[]{:S(2)}, u32[]{:S(2)}) collective-permute-start(f32[3,3,1,3,128]{4,3,2,1,0:T(4,128)S(1)} %pad_maximum_fusion.9), channel_id=1, source_target_pairs={{1,0},{2,1},{3,2},{4,3},{5,4},{6,5},{7,6},{8,7},{9,8},{10,9},{11,1... | collective-permute-start | bytes 41480 | tf_op jit(solution)/shard_map/ppermute | solution.py:20
  252.8 11.9 %collective-permute-done.22 = f32[3,3,1,3,128]{4,3,2,1,0:T(4,128)S(1)} collective-permute-done((f32[3,3,1,3,128]{4,3,2,1,0:T(4,128)S(1)}, f32[3,3,1,3,128]{4,3,2,1,0:T(4,128)S(1)}, u32[]{:S(2)}, u32[]{:S(2)}) %collective-permute-start.22) | collective-permute-done | bytes 13856 | tf_op jit(solution)/shard_map/ppermute | solution.py:19
  268.6 24.4 %while.32 = (s32[]{:T(128)}, f32[6,128,256]{2,1,0:T(8,128)S(1)}, f32[128,256]{1,0:T(8,128)S(1)}, s32[3]{0:T(128)S(1)}, bf16[3,9,128,1152]{3,2,1,0:T(8,128)(2,1)}...) while((s32[]{:T(128)}, f32[6,128,256]{2,1,0:T(8,128)S(1)}, ...), condition=%wide.region_3.4_spmd.clone, body=%wide.region_2.3_spmd.clone.sunk | while | flops 530268160 | bytes 9249608 | solution.py:119
  (145 shorter events, 93.2 us)
Async XLA Ops:
  2.5 16.9 %collective-permute-start.7 = (bf16[1,1,1,128,256]{4,3,2,1,0:T(8,128)(2,1)S(1)}, bf16[1,1,1,128,256]{4,3,2,1,0:T(8,128)(2,1)S(1)}, u32[]{:S(2)}, u32[]{:S(2)}) collective-permute-start(bf16[1,1,1,128,256]{4,3,2,1,0:T(8,128)(2,1)S(1)} %fusion.43), channel_id=1, source_target_pairs={{256,0},{512,256},{768,512},{0,768},{257,1},{513,257},{769,513},{1... | collective-permute-start | bytes 196616 | tf_op jit(solution)/shard_map/ppermute | solution.py:20
  17.6 6.2 %collective-permute-start.6 = (bf16[1,1,1,128,256]{4,3,2,1,0:T(8,128)(2,1)S(1)}, bf16[1,1,1,128,256]{4,3,2,1,0:T(8,128)(2,1)S(1)}, u32[]{:S(2)}, u32[]{:S(2)}) collective-permute-start(bf16[1,1,1,128,256]{4,3,2,1,0:T(8,128)(2,1)S(1)} %fusion.43), channel_id=1, source_target_pairs={{0,256},{256,512},{512,768},{768,0},{1,257},{257,513},{513,769},{7... | collective-permute-start | bytes 196616 | tf_op jit(solution)/shard_map/ppermute | solution.py:19
  23.7 27.8 %collective-permute-start.9 = (bf16[3,1,1,128,256]{4,3,2,1,0:T(8,128)(2,1)S(1)}, bf16[3,1,1,128,256]{4,3,2,1,0:T(8,128)(2,1)S(1)}, u32[]{:S(2)}, u32[]{:S(2)}) collective-permute-start(bf16[3,1,1,128,256]{4,3,2,1,0:T(8,128)(2,1)S(1)} %pad_maximum_fusion.5), channel_id=1, source_target_pairs={{32,0},{64,32},{96,64},{128,96},{160,128},{192,160},{224,192},{0,2... | collective-permute-start | bytes 589832 | tf_op jit(solution)/shard_map/ppermute | solution.py:20
  33.4 30.1 %collective-permute-start.8 = (bf16[3,1,1,128,256]{4,3,2,1,0:T(8,128)(2,1)S(1)}, bf16[3,1,1,128,256]{4,3,2,1,0:T(8,128)(2,1)S(1)}, u32[]{:S(2)}, u32[]{:S(2)}) collective-permute-start(bf16[3,1,1,128,256]{4,3,2,1,0:T(8,128)(2,1)S(1)} %pad_maximum_fusion.5), channel_id=1, source_target_pairs={{0,32},{32,64},{64,96},{96,128},{128,160},{160,192},{192,224},{224... | collective-permute-start | bytes 589832 | tf_op jit(solution)/shard_map/ppermute | solution.py:19
  63.6 62.9 %collective-permute-start.11 = (bf16[3,3,1,128,256]{4,3,2,1,0:T(8,128)(2,1)S(1)}, bf16[3,3,1,128,256]{4,3,2,1,0:T(8,128)(2,1)S(1)}, u32[]{:S(2)}, u32[]{:S(2)}) collective-permute-start(bf16[3,3,1,128,256]{4,3,2,1,0:T(8,128)(2,1)S(1)} %pad_maximum_fusion.3), channel_id=1, source_target_pairs={{1,0},{2,1},{3,2},{4,3},{5,4},{6,5},{7,6},{8,7},{9,8},{10,9},{11,1... | collective-permute-start | bytes 1769480 | tf_op jit(solution)/shard_map/ppermute | solution.py:20
  71.6 54.9 %collective-permute-start.10 = (bf16[3,3,1,128,256]{4,3,2,1,0:T(8,128)(2,1)S(1)}, bf16[3,3,1,128,256]{4,3,2,1,0:T(8,128)(2,1)S(1)}, u32[]{:S(2)}, u32[]{:S(2)}) collective-permute-start(bf16[3,3,1,128,256]{4,3,2,1,0:T(8,128)(2,1)S(1)} %pad_maximum_fusion.3), channel_id=1, source_target_pairs={{0,1},{1,2},{2,3},{3,4},{4,5},{5,6},{6,7},{7,8},{8,9},{9,10},{10,1... | collective-permute-start | bytes 1769480 | tf_op jit(solution)/shard_map/ppermute | solution.py:19
  73.5 6.8 %collective-permute-start.1 = (f32[1,1,1,4,128]{4,3,2,1,0:T(4,128)S(1)}, f32[1,1,1,4,128]{4,3,2,1,0:T(4,128)S(1)}, u32[]{:S(2)}, u32[]{:S(2)}) collective-permute-start(f32[1,1,1,4,128]{4,3,2,1,0:T(4,128)S(1)} %maximum_bitcast_fusion.1), channel_id=1, source_target_pairs={{256,0},{512,256},{768,512},{0,768},{257,1},{513,257},{769,513},{1... | collective-permute-start | bytes 6152 | tf_op jit(solution)/shard_map/ppermute | solution.py:20
  78.4 5.5 %collective-permute-start = (f32[1,1,1,4,128]{4,3,2,1,0:T(4,128)S(1)}, f32[1,1,1,4,128]{4,3,2,1,0:T(4,128)S(1)}, u32[]{:S(2)}, u32[]{:S(2)}) collective-permute-start(f32[1,1,1,4,128]{4,3,2,1,0:T(4,128)S(1)} %maximum_bitcast_fusion.1), channel_id=1, source_target_pairs={{0,256},{256,512},{512,768},{768,0},{1,257},{257,513},{513,769},{7... | collective-permute-start | bytes 6152 | tf_op jit(solution)/shard_map/ppermute | solution.py:19
  83.9 4.3 %collective-permute-start.3 = (f32[3,1,1,4,128]{4,3,2,1,0:T(4,128)S(1)}, f32[3,1,1,4,128]{4,3,2,1,0:T(4,128)S(1)}, u32[]{:S(2)}, u32[]{:S(2)}) collective-permute-start(f32[3,1,1,4,128]{4,3,2,1,0:T(4,128)S(1)} %pad_maximum_fusion.10), channel_id=1, source_target_pairs={{32,0},{64,32},{96,64},{128,96},{160,128},{192,160},{224,192},{0,2... | collective-permute-start | bytes 18440 | tf_op jit(solution)/shard_map/ppermute | solution.py:20
  85.8 13.7 %collective-permute-start.2 = (f32[3,1,1,4,128]{4,3,2,1,0:T(4,128)S(1)}, f32[3,1,1,4,128]{4,3,2,1,0:T(4,128)S(1)}, u32[]{:S(2)}, u32[]{:S(2)}) collective-permute-start(f32[3,1,1,4,128]{4,3,2,1,0:T(4,128)S(1)} %pad_maximum_fusion.10), channel_id=1, source_target_pairs={{0,32},{32,64},{64,96},{96,128},{128,160},{160,192},{192,224},{224... | collective-permute-start | bytes 18440 | tf_op jit(solution)/shard_map/ppermute | solution.py:19
  99.4 14.6 %collective-permute-start.5 = (f32[3,3,1,4,128]{4,3,2,1,0:T(4,128)S(1)}, f32[3,3,1,4,128]{4,3,2,1,0:T(4,128)S(1)}, u32[]{:S(2)}, u32[]{:S(2)}) collective-permute-start(f32[3,3,1,4,128]{4,3,2,1,0:T(4,128)S(1)} %pad_maximum_fusion.8), channel_id=1, source_target_pairs={{1,0},{2,1},{3,2},{4,3},{5,4},{6,5},{7,6},{8,7},{9,8},{10,9},{11,1... | collective-permute-start | bytes 55304 | tf_op jit(solution)/shard_map/ppermute | solution.py:20
  112.1 14.4 %collective-permute-start.4 = (f32[3,3,1,4,128]{4,3,2,1,0:T(4,128)S(1)}, f32[3,3,1,4,128]{4,3,2,1,0:T(4,128)S(1)}, u32[]{:S(2)}, u32[]{:S(2)}) collective-permute-start(f32[3,3,1,4,128]{4,3,2,1,0:T(4,128)S(1)} %pad_maximum_fusion.8), channel_id=1, source_target_pairs={{0,1},{1,2},{2,3},{3,4},{4,5},{5,6},{6,7},{7,8},{8,9},{9,10},{10,1... | collective-permute-start | bytes 55304 | tf_op jit(solution)/shard_map/ppermute | solution.py:19
  170.7 6.9 %collective-permute-start.13 = (bf16[1,1,1,128,512]{4,3,2,1,0:T(8,128)(2,1)S(1)}, bf16[1,1,1,128,512]{4,3,2,1,0:T(8,128)(2,1)S(1)}, u32[]{:S(2)}, u32[]{:S(2)}) collective-permute-start(bf16[1,1,1,128,512]{4,3,2,1,0:T(8,128)(2,1)S(1)} %maximum_bitcast_fusion), channel_id=1, source_target_pairs={{256,0},{512,256},{768,512},{0,768},{257,1},{513,257},{769,513},{1... | collective-permute-start | bytes 393224 | tf_op jit(solution)/shard_map/ppermute | solution.py:20
  173.8 6.9 %collective-permute-start.12 = (bf16[1,1,1,128,512]{4,3,2,1,0:T(8,128)(2,1)S(1)}, bf16[1,1,1,128,512]{4,3,2,1,0:T(8,128)(2,1)S(1)}, u32[]{:S(2)}, u32[]{:S(2)}) collective-permute-start(bf16[1,1,1,128,512]{4,3,2,1,0:T(8,128)(2,1)S(1)} %maximum_bitcast_fusion), channel_id=1, source_target_pairs={{0,256},{256,512},{512,768},{768,0},{1,257},{257,513},{513,769},{7... | collective-permute-start | bytes 393224 | tf_op jit(solution)/shard_map/ppermute | solution.py:19
  180.8 13.9 %collective-permute-start.15 = (bf16[3,1,1,128,512]{4,3,2,1,0:T(8,128)(2,1)S(1)}, bf16[3,1,1,128,512]{4,3,2,1,0:T(8,128)(2,1)S(1)}, u32[]{:S(2)}, u32[]{:S(2)}) collective-permute-start(bf16[3,1,1,128,512]{4,3,2,1,0:T(8,128)(2,1)S(1)} %pad_maximum_fusion.4), channel_id=1, source_target_pairs={{32,0},{64,32},{96,64},{128,96},{160,128},{192,160},{224,192},{0,2... | collective-permute-start | bytes 1179656 | tf_op jit(solution)/shard_map/ppermute | solution.py:20
  182.7 25.6 %collective-permute-start.14 = (bf16[3,1,1,128,512]{4,3,2,1,0:T(8,128)(2,1)S(1)}, bf16[3,1,1,128,512]{4,3,2,1,0:T(8,128)(2,1)S(1)}, u32[]{:S(2)}, u32[]{:S(2)}) collective-permute-start(bf16[3,1,1,128,512]{4,3,2,1,0:T(8,128)(2,1)S(1)} %pad_maximum_fusion.4), channel_id=1, source_target_pairs={{0,32},{32,64},{64,96},{96,128},{128,160},{160,192},{192,224},{224... | collective-permute-start | bytes 1179656 | tf_op jit(solution)/shard_map/ppermute | solution.py:19
  209.5 55.1 %collective-permute-start.17 = (bf16[3,3,1,128,512]{4,3,2,1,0:T(8,128)(2,1)}, bf16[3,3,1,128,512]{4,3,2,1,0:T(8,128)(2,1)}, u32[]{:S(2)}, u32[]{:S(2)}) collective-permute-start(bf16[3,3,1,128,512]{4,3,2,1,0:T(8,128)(2,1)} %pad_maximum_fusion.2), channel_id=1, source_target_pairs={{1,0},{2,1},{3,2},{4,3},{5,4},{6,5},{7,6},{8,7},{9,8},{10,9},{11,1... | collective-permute-start | bytes 3538952 | tf_op jit(solution)/shard_map/ppermute | solution.py:20
  211.5 53.2 %collective-permute-start.16 = (bf16[3,3,1,128,512]{4,3,2,1,0:T(8,128)(2,1)}, bf16[3,3,1,128,512]{4,3,2,1,0:T(8,128)(2,1)}, u32[]{:S(2)}, u32[]{:S(2)}) collective-permute-start(bf16[3,3,1,128,512]{4,3,2,1,0:T(8,128)(2,1)} %pad_maximum_fusion.2), channel_id=1, source_target_pairs={{0,1},{1,2},{2,3},{3,4},{4,5},{5,6},{6,7},{7,8},{8,9},{9,10},{10,1... | collective-permute-start | bytes 3538952 | tf_op jit(solution)/shard_map/ppermute | solution.py:19
  215.4 5.9 %collective-permute-start.19 = (f32[1,1,1,3,128]{4,3,2,1,0:T(4,128)S(1)}, f32[1,1,1,3,128]{4,3,2,1,0:T(4,128)S(1)}, u32[]{:S(2)}, u32[]{:S(2)}) collective-permute-start(f32[1,1,1,3,128]{4,3,2,1,0:T(4,128)S(1)} %get-tuple-element.370), channel_id=1, source_target_pairs={{256,0},{512,256},{768,512},{0,768},{257,1},{513,257},{769,513},{1... | collective-permute-start | bytes 4616 | tf_op jit(solution)/shard_map/ppermute | solution.py:20
  218.5 5.5 %collective-permute-start.18 = (f32[1,1,1,3,128]{4,3,2,1,0:T(4,128)S(1)}, f32[1,1,1,3,128]{4,3,2,1,0:T(4,128)S(1)}, u32[]{:S(2)}, u32[]{:S(2)}) collective-permute-start(f32[1,1,1,3,128]{4,3,2,1,0:T(4,128)S(1)} %get-tuple-element.370), channel_id=1, source_target_pairs={{0,256},{256,512},{512,768},{768,0},{1,257},{257,513},{513,769},{7... | collective-permute-start | bytes 4616 | tf_op jit(solution)/shard_map/ppermute | solution.py:19
  224.0 4.3 %collective-permute-start.21 = (f32[3,1,1,3,128]{4,3,2,1,0:T(4,128)S(1)}, f32[3,1,1,3,128]{4,3,2,1,0:T(4,128)S(1)}, u32[]{:S(2)}, u32[]{:S(2)}) collective-permute-start(f32[3,1,1,3,128]{4,3,2,1,0:T(4,128)S(1)} %pad_maximum_fusion.11), channel_id=1, source_target_pairs={{32,0},{64,32},{96,64},{128,96},{160,128},{192,160},{224,192},{0,2... | collective-permute-start | bytes 13832 | tf_op jit(solution)/shard_map/ppermute | solution.py:20
  225.9 13.7 %collective-permute-start.20 = (f32[3,1,1,3,128]{4,3,2,1,0:T(4,128)S(1)}, f32[3,1,1,3,128]{4,3,2,1,0:T(4,128)S(1)}, u32[]{:S(2)}, u32[]{:S(2)}) collective-permute-start(f32[3,1,1,3,128]{4,3,2,1,0:T(4,128)S(1)} %pad_maximum_fusion.11), channel_id=1, source_target_pairs={{0,32},{32,64},{64,96},{96,128},{128,160},{160,192},{192,224},{224... | collective-permute-start | bytes 13832 | tf_op jit(solution)/shard_map/ppermute | solution.py:19
  239.6 13.1 %collective-permute-start.23 = (f32[3,3,1,3,128]{4,3,2,1,0:T(4,128)S(1)}, f32[3,3,1,3,128]{4,3,2,1,0:T(4,128)S(1)}, u32[]{:S(2)}, u32[]{:S(2)}) collective-permute-start(f32[3,3,1,3,128]{4,3,2,1,0:T(4,128)S(1)} %pad_maximum_fusion.9), channel_id=1, source_target_pairs={{1,0},{2,1},{3,2},{4,3},{5,4},{6,5},{7,6},{8,7},{9,8},{10,9},{11,1... | collective-permute-start | bytes 41480 | tf_op jit(solution)/shard_map/ppermute | solution.py:20
  250.2 14.4 %collective-permute-start.22 = (f32[3,3,1,3,128]{4,3,2,1,0:T(4,128)S(1)}, f32[3,3,1,3,128]{4,3,2,1,0:T(4,128)S(1)}, u32[]{:S(2)}, u32[]{:S(2)}) collective-permute-start(f32[3,3,1,3,128]{4,3,2,1,0:T(4,128)S(1)} %pad_maximum_fusion.9), channel_id=1, source_target_pairs={{0,1},{1,2},{2,3},{3,4},{4,5},{5,6},{6,7},{7,8},{8,9},{9,10},{10,1... | collective-permute-start | bytes 41480 | tf_op jit(solution)/shard_map/ppermute | solution.py:19
  (5 other events, 196.6 us)
where the time goes:
time: 295 us; the launch traced here: 294 us
  waiting for transfers between devices  111 us (38%)
  starting transfers between devices  103 us (35%)
  other arithmetic  29.3 us (10%)
  matrix products  28.3 us (10%)
  loops' own time  11.1 us (4%)
  local copies, waits for them, and re-layouts  9.36 us (3%)
    ppermute x12, waiting for transfers between devices, padded(): before = lax.ppermute(last, axis, up)  86 us
    ppermute x12, starting transfers between devices, padded(): after = lax.ppermute(leading, axis, down)  74.7 us
    ppermute x12, starting transfers between devices, padded(): before = lax.ppermute(last, axis, up)  28.1 us
    ppermute x12, waiting for transfers between devices, padded(): after = lax.ppermute(leading, axis, down)  25.4 us
    dot_general x3, matrix products, forward_plane(): jnp.einsum('kij,jf->kif', kern, block, preferred_element_type=jnp.float32)  12.4 us
    concatenate x6, other arithmetic, build_kernels(): jnp.concatenate([radial_part, direction_part], 0).astype(jnp.bfloat16)  10.2 us
    dot_general x3, matrix products, backward_plane(): jnp.einsum('bij,jf->bif', kern[:bases], slope_block, preferred_element_ty...  7.43 us
    another operation x1, loops' own time, on_device(): lax.scan(backward_plane, begin, jnp.arange(3, dtype=jnp.int32))  6.93 us
  transfers between devices with their start and end apart: 24, of which 13 were waited for; matrix products, arithmetic and copies ran while one was open for 0% of the time, Pallas kernels for 0%

commit v1 on v0

v1 whole, which is shorter than its diff:
```python
import math

import jax
import jax.numpy as jnp
from jax import lax
from jax.experimental import pallas as pl
from jax.experimental.pallas import tpu as pltpu
from jax.sharding import PartitionSpec as P

EDGE = 10.0
CUT = 5.0
GAMMA = 20.0
LOSS_WEIGHT = 16.0
FAR_AWAY = 1.0e4
MESH = pl.DeviceIdType.MESH
ROWS = 32

OWN, SIB, FAR = 0, 1, 2
STEPS = (0, -1, 1)
TARGETS = ((FAR, 1), (FAR, 2), (SIB, 1), (SIB, 2), (SIB, 0), (OWN, 1), (OWN, 2), (FAR, 0), (OWN, 0))


def slot(a, role, c):
    return role * 9 + a * 3 + c


def kernel(
    count_ref, offs_ref, feat_ref, mask_ref, targ_ref, w_ref, radial_ref, readout_ref,
    back_ref, pred_ref,
    proj, coords, rows_j, cols_i, kern_f, kern_b, msg, rhs, partial, acts, errs, zcols,
    part_sib, got_sib, part_gz, got_gz, part_far, got_far, send_sem, recv_sem,
):
    atoms, width = feat_ref.shape
    bases = radial_ref.shape[0]
    kinds = bases + 3
    f32, bf16 = jnp.float32, jnp.bfloat16
    gx, gy, gz = lax.axis_index("gx"), lax.axis_index("gy"), lax.axis_index("gz")
    nx, ny, nz = lax.axis_size("gx"), lax.axis_size("gy"), lax.axis_size("gz")
    core = gy % 2
    sib_gy = gy + 1 - 2 * core
    far_gy = (gy + ny - 1 + 2 * core) % ny
    sib = (gx, sib_gy, gz)
    far = (gx, far_gy, gz)
    to_gx = {1: ((gx + nx - 1) % nx, gy, gz), 2: ((gx + 1) % nx, gy, gz)}
    to_gz = {1: (gx, gy, (gz + nz - 1) % nz), 2: (gx, gy, (gz + 1) % nz)}
    flip = {1: 2, 2: 1}
    sib_step = (1 - 2 * core).astype(f32)
    role_step = (0.0, sib_step, -sib_step)

    barrier = pltpu.get_barrier_semaphore()
    for other in (far, to_gz[1], to_gz[2], to_gx[1], to_gx[2], sib):
        pl.semaphore_signal(barrier, inc=1, device_id=other, device_id_type=MESH)

    copies = {}

    def send(name, src, dst, device):
        index = len(copies)
        copy = pltpu.make_async_remote_copy(
            src_ref=src, dst_ref=dst, send_sem=send_sem.at[index], recv_sem=recv_sem.at[index],
            device_id=device, device_id_type=MESH,
        )
        copies[name] = copy
        copy.start()

    def wait(name):
        copies[name].wait_recv()

    def send_proj(a, role, c, to):
        here = proj.at[slot(a, role, c)]
        kind, d = to
        if kind == "sib":
            send(("p", a, SIB, c), here, proj.at[slot(a, SIB, c)], sib)
        elif kind == "far":
            send(("p", a, FAR, c), here, proj.at[slot(a, FAR, c)], far)
        elif kind == "gz":
            send(("p", a, role, flip[d]), here, proj.at[slot(a, role, flip[d])], to_gz[d])
        else:
            send(("p", flip[d], role, c), here, proj.at[slot(flip[d], role, c)], to_gx[d])

    lane = lax.broadcasted_iota(jnp.int32, (1, atoms), 1)
    occ_row = lane < count_ref[0]
    own = offs_ref[...] * (1.0 / CUT)
    coords[0, 0, OWN] = jnp.concatenate(
        [jnp.where(occ_row, own[0:1], FAR_AWAY), own[1:3], jnp.zeros((5, atoms), f32)], 0
    )
    proj[slot(0, OWN, 0)] = jnp.dot(
        feat_ref[...], w_ref[...], preferred_element_type=f32
    ).astype(bf16)

    pl.semaphore_wait(barrier, 6)

    send("c_far", coords.at[0, 0, OWN], coords.at[0, 0, FAR], far)
    send_proj(0, OWN, 0, ("far", 0))
    for d in (1, 2):
        send_proj(0, OWN, 0, ("gz", d))
    send("c_sib", coords.at[0, 0, OWN], coords.at[0, 0, SIB], sib)
    send_proj(0, OWN, 0, ("sib", 0))
    for d in (1, 2):
        send_proj(0, OWN, 0, ("gx", d))

    row_id = lax.broadcasted_iota(jnp.int32, (ROWS, atoms), 0)
    col_id = lax.broadcasted_iota(jnp.int32, (ROWS, atoms), 1)
    step = 2.0 * EDGE / (2.0 * CUT)

    def fill(block, xi, yi, zi, store, diag=None):
        dx = block[0:1] - xi
        dy = block[1:2] - yi
        dz = block[2:3] - zi
        ratio = dx * dx + dy * dy + dz * dz
        if diag is not None:
            ratio = ratio + diag
        room = jnp.maximum(1.0 - ratio, 0.0)
        near = 1.0 - room
        env = room * room
        grow = jnp.exp((2.0 * GAMMA / (bases - 1)) * near)
        value = env * jnp.exp(-GAMMA * (near * near))
        for k in range(bases):
            store(k, value.astype(bf16))
            if k < bases - 1:
                value = value * grow
        store(bases, (env * dx).astype(bf16))
        store(bases + 1, (env * dy).astype(bf16))
        store(bases + 2, (env * dz).astype(bf16))

    def place_rows(a, role, c):
        block = coords[a, c, role]
        r8 = lax.broadcasted_iota(jnp.int32, block.shape, 0)
        shift = jnp.where(
            r8 == 0, step * STEPS[a],
            jnp.where(r8 == 1, step * role_step[role], jnp.where(r8 == 2, step * STEPS[c], 0.0)),
        )
        rows_j[slot(a, role, c)] = block + shift

    def place_cols(blocks):
        stack = []
        for role, c in blocks:
            block = rows_j[slot(0, role, c)]
            r8 = lax.broadcasted_iota(jnp.int32, block.shape, 0)
            stack.append(jnp.where((r8 == 0) & (block > 0.5 * FAR_AWAY), -FAR_AWAY, block))
        if len(stack) < 16:
            stack.append(jnp.zeros((8 * (16 - len(stack)), atoms), f32))
        turned = jnp.transpose(jnp.concatenate(stack, 0))
        for n, where in enumerate(blocks):
            t = TARGETS.index(where)
            for axis in range(3):
                cols_i[t, axis] = jnp.broadcast_to(
                    turned[:, 8 * n + axis : 8 * n + axis + 1], (atoms, atoms)
                )

    own_t = TARGETS.index((OWN, 0))

    def forward_slots(slots, diag=False):
        for q in range(atoms // ROWS):
            at = slice(q * ROWS, (q + 1) * ROWS)
            xi, yi, zi = cols_i[own_t, 0, at], cols_i[own_t, 1, at], cols_i[own_t, 2, at]
            eye = jnp.where(row_id + q * ROWS == col_id, 4.0, 0.0) if diag else None
            for first, count, stride in slots:

                def one(n, unused, at=at, xi=xi, yi=yi, zi=zi, first=first, stride=stride, eye=eye):
                    s = first + n * stride
                    lanes = pl.ds(pl.multiple_of(s * atoms, atoms), atoms)

                    def store(k, value):
                        kern_f[k, at, lanes] = value

                    fill(rows_j[s], xi, yi, zi, store, eye)
                    return unused

                lax.fori_loop(0, count, one, 0)

    def backward_blocks(first, count, sources, diag=False):
        def one(n, unused):
            t = first + n // (atoms // ROWS)
            q = n % (atoms // ROWS)
            at = pl.ds(pl.multiple_of(q * ROWS, ROWS), ROWS)
            xi, yi, zi = cols_i[t, 0, at], cols_i[t, 1, at], cols_i[t, 2, at]
            eye = jnp.where(row_id + q * ROWS == col_id, 4.0, 0.0) if diag else None
            for a in sources:

                def store(k, value, a=a):
                    lo = (a * kinds + k) * atoms
                    kern_b[t, at, lo : lo + atoms] = value

                fill(rows_j[slot(a, OWN, 0)], xi, yi, zi, store, eye)
            return unused

        lax.fori_loop(0, count * (atoms // ROWS), one, 0)

    place_rows(0, OWN, 0)
    place_cols([(OWN, 0)])
    forward_slots([(slot(0, OWN, 0), 1, 1)], diag=True)

    wait("c_sib")
    wait(("p", 0, SIB, 0))
    for a in (1, 2):
        wait(("p", a, OWN, 0))
        send_proj(a, OWN, 0, ("sib", 0))
    wait("c_far")
    for d in (1, 2):
        send(("c_gz", flip[d]), coords.at[0, 0], coords.at[0, flip[d]], to_gz[d])
    place_rows(0, SIB, 0)
    place_rows(0, FAR, 0)
    forward_slots([(slot(0, SIB, 0), 2, 9)])
    for c in (1, 2):
        wait(("p", 0, OWN, c))
        for d in (1, 2):
            send_proj(0, OWN, c, ("gx", d))
        send_proj(0, OWN, c, ("sib", 0))
    wait(("p", 0, FAR, 0))
    for d in (1, 2):
        send_proj(0, FAR, 0, ("gz", d))
    for d in (1, 2):
        send_proj(0, FAR, 0, ("gx", d))
    for c in (1, 2):
        wait(("c_gz", c))
    for d in (1, 2):
        send(("c_gx", flip[d]), coords.at[0], coords.at[flip[d]], to_gx[d])
    for a in (1, 2):
        for c in (1, 2):
            wait(("p", a, OWN, c))
            send_proj(a, OWN, c, ("sib", 0))
    for role in (OWN, SIB, FAR):
        for c in (1, 2):
            place_rows(0, role, c)
    forward_slots([(slot(0, role, 1), 2, 1) for role in (OWN, SIB, FAR)])
    for c in (1, 2):
        wait(("p", 0, FAR, c))
        for d in (1, 2):
            send_proj(0, FAR, c, ("gx", d))
    for a in (1, 2):
        wait(("c_gx", a))
        for role in (OWN, SIB, FAR):
            for c in (0, 1, 2):
                place_rows(a, role, c)
    forward_slots([(slot(1, role, 0), 6, 1) for role in (OWN, SIB, FAR)])
    place_cols(list(TARGETS))
    backward_blocks(0, 8, (0, 1, 2))
    backward_blocks(8, 1, (0,), diag=True)
    backward_blocks(8, 1, (1, 2))

    for a in (0, 1, 2):
        for c in (0, 1, 2):
            if (a, c) != (0, 0):
                wait(("p", a, SIB, c))
    near = 18 * atoms
    msg[...] = jnp.dot(
        kern_f[:, :, :near].reshape(kinds * atoms, near),
        proj[0:18].reshape(near, width),
        preferred_element_type=f32,
    ).reshape(kinds, atoms, width)
    for a in (1, 2):
        for c in (0, 1, 2):
            wait(("p", a, FAR, c))
    msg[...] = msg[...] + jnp.dot(
        kern_f[:, :, near:].reshape(kinds * atoms, 9 * atoms),
        proj[18:27].reshape(9 * atoms, width),
        preferred_element_type=f32,
    ).reshape(kinds, atoms, width)

    weights = [
        radial_ref[b : b + 1] * math.exp(-GAMMA * (b / (bases - 1)) ** 2) for b in range(bases)
    ]
    readout = readout_ref[...]
    info = jnp.concatenate(
        [
            targ_ref[...],
            jnp.where(occ_row, mask_ref[...].astype(f32) * LOSS_WEIGHT, 0.0),
            jnp.zeros((atoms - 4, atoms), f32),
        ],
        0,
    )
    zcols[...] = jnp.transpose(info)
    for q in range(atoms // ROWS):
        at = slice(q * ROWS, (q + 1) * ROWS)
        pre = weights[0] * msg[0, at]
        for b in range(1, bases):
            pre = pre + weights[b] * msg[b, at]
        gate = jax.nn.sigmoid(pre)
        gates = readout * gate
        cols = zcols[at]
        scale = cols[:, 3:4]
        pull = jnp.zeros_like(pre)
        out = jnp.zeros((ROWS, atoms), f32)
        for c in range(3):
            vec = msg[bases + c, at]
            pred = jnp.sum(gates * vec, axis=1, keepdims=True)
            err = scale * (pred - cols[:, c : c + 1])
            pull = pull + err * vec
            out = jnp.where(col_id == c, pred, out)
            out = jnp.where(col_id == 3 + c, err, out)
        zcols[at] = out
        acts[0, 0, at] = (pull * readout * gate * (1.0 - gate)).astype(bf16)
        acts[0, 1, at] = gates.astype(bf16)
    turned = jnp.transpose(zcols[...])
    pred_ref[...] = turned[0:8]
    errs[0] = turned[0:8]

    for d in (1, 2):
        send(("act", flip[d]), acts.at[0], acts.at[flip[d]], to_gx[d])
        send(("err", flip[d]), errs.at[0], errs.at[flip[d]], to_gx[d])

    def build_rhs(a, cols, first):
        for q in range(atoms // ROWS):
            at = slice(q * ROWS, (q + 1) * ROWS)
            slope = acts[a, 0, at].astype(f32)
            gates = acts[a, 1, at].astype(f32)
            for b in range(bases):
                rhs[a * kinds + b, at] = (weights[b] * slope).astype(bf16)
            for c in range(3):
                err = cols[q * ROWS : (q + 1) * ROWS, first + c : first + c + 1]
                rhs[a * kinds + bases + c, at] = (gates * (-err)).astype(bf16)

    build_rhs(0, zcols[...], 3)
    part = kinds * atoms
    partial[...] = jnp.dot(
        kern_b[:, :, :part].reshape(9 * atoms, part),
        rhs[0:kinds].reshape(part, width),
        preferred_element_type=f32,
    ).reshape(9, atoms, width)
    for a in (1, 2):
        wait(("act", a))
        wait(("err", a))
    zcols[...] = jnp.transpose(
        jnp.concatenate([errs[1], errs[2], jnp.zeros((atoms - 16, atoms), f32)], 0)
    )
    build_rhs(1, zcols[...], 3)
    build_rhs(2, zcols[...], 11)

    def totals(first, count):
        return partial[first : first + count] + jnp.dot(
            kern_b[first : first + count, :, part:].reshape(count * atoms, 2 * part),
            rhs[kinds:].reshape(2 * part, width),
            preferred_element_type=f32,
        ).reshape(count, atoms, width)

    part_gz[1] = totals(0, 2).astype(bf16)
    for d in (1, 2):
        send(("far_gz", flip[d]), part_gz.at[1, d - 1], got_gz.at[1, flip[d] - 1], to_gz[d])
    part_sib[...] = totals(2, 3).astype(bf16)
    send("sib", part_sib, got_sib, sib)
    partial[5:7] = totals(5, 2)
    wait("sib")
    part_gz[0] = (partial[5:7] + got_sib[0:2].astype(f32)).astype(bf16)
    for d in (1, 2):
        send(("own_gz", flip[d]), part_gz.at[0, d - 1], got_gz.at[0, flip[d] - 1], to_gz[d])
    partial[7:9] = totals(7, 2)
    for c in (1, 2):
        wait(("far_gz", c))
    part_far[...] = (
        partial[7] + got_gz[1, 0].astype(f32) + got_gz[1, 1].astype(f32)
    ).astype(bf16)
    send("far", part_far, got_far, far)
    for c in (1, 2):
        wait(("own_gz", c))
    total = partial[8] + got_sib[2].astype(f32)
    total = total + got_gz[0, 0].astype(f32) + got_gz[0, 1].astype(f32)
    wait("far")
    back_ref[...] = (total + got_far[...].astype(f32)).astype(bf16)
    for copy in copies.values():
        copy.wait_send()


COPIES = 26 + 6 + 4 + 6


def on_device(offsets, features, counts, mask, targets, w_in, radial, readout):
    atoms, width = features.shape[3:]
    bases = radial.shape[0]
    kinds = bases + 3
    f32, bf16 = jnp.float32, jnp.bfloat16
    vmem = pl.BlockSpec(memory_space=pltpu.VMEM)
    back, pred = pl.pallas_call(
        kernel,
        out_shape=(
            jax.ShapeDtypeStruct((atoms, width), bf16),
            jax.ShapeDtypeStruct((8, atoms), f32),
        ),
        in_specs=[pl.BlockSpec(memory_space=pltpu.SMEM)] + [vmem] * 7,
        out_specs=(vmem, vmem),
        scratch_shapes=[
            pltpu.VMEM((27, atoms, width), bf16),
            pltpu.VMEM((3, 3, 3, 8, atoms), f32),
            pltpu.VMEM((27, 8, atoms), f32),
            pltpu.VMEM((9, 3, atoms, atoms), f32),
            pltpu.VMEM((kinds, atoms, 27 * atoms), bf16),
            pltpu.VMEM((9, atoms, 3 * kinds * atoms), bf16),
            pltpu.VMEM((kinds, atoms, width), f32),
            pltpu.VMEM((3 * kinds, atoms, width), bf16),
            pltpu.VMEM((9, atoms, width), f32),
            pltpu.VMEM((3, 2, atoms, width), bf16),
            pltpu.VMEM((3, 8, atoms), f32),
            pltpu.VMEM((atoms, atoms), f32),
            pltpu.VMEM((3, atoms, width), bf16),
            pltpu.VMEM((3, atoms, width), bf16),
            pltpu.VMEM((2, 2, atoms, width), bf16),
            pltpu.VMEM((2, 2, atoms, width), bf16),
            pltpu.VMEM((atoms, width), bf16),
            pltpu.VMEM((atoms, width), bf16),
            pltpu.SemaphoreType.DMA((COPIES,)),
            pltpu.SemaphoreType.DMA((COPIES,)),
        ],
        compiler_params=pltpu.CompilerParams(
            collective_id=0, has_side_effects=True, vmem_limit_bytes=48 << 20
        ),
        name="message_passing",
    )(
        counts.reshape(1),
        offsets.reshape(3, atoms),
        features.reshape(atoms, width),
        mask.reshape(1, atoms),
        targets.reshape(3, atoms),
        w_in,
        radial,
        readout.reshape(1, width),
    )
    grad = lax.dot_general(
        back, w_in, (((1,), (1,)), ((), ())), preferred_element_type=jnp.float32
    )
    return (pred[0:3].reshape(1, 1, 1, 3, atoms), grad.reshape(1, 1, 1, atoms, width))


def solution(mesh):
    in_specs = (
        P("gx", "gy", "gz", None, None),
        P("gx", "gy", "gz", None, None),
        P("gx", "gy", "gz"),
        P("gx", "gy", "gz", None),
        P("gx", "gy", "gz", None, None),
        P(),
        P(),
        P(),
    )
    out_specs = (P("gx", "gy", "gz", None, None), P("gx", "gy", "gz", None, None))
    return jax.shard_map(
        on_device, mesh=mesh, in_specs=in_specs, out_specs=out_specs, check_vma=False
    )
```

time: 295 us -> 80.5 us (0.27)
  the two profiles are of different devices: /device:TPU:8 before, /device:TPU:1 now
where the time goes in v1:
time: 80.5 us; the launch traced here: 80.2 us
  Pallas kernels  74.4 us (92%)
  local copies, waits for them, and re-layouts  3.67 us (5%)
  between operations  1.32 us (2%)
  matrix products  0.86 us (1%)
    pallas_call x1, Pallas kernels, on_device(): pl.pallas_call(kernel, out_shape=(jax.ShapeDtypeStruct((atoms, width), bf...  74.4 us
    unnamed x16, local copies, waits for them, and re-layouts  3.66 us

profile of v1, /device:TPU:1, one launch (start us, length us, event | category | flops | bytes accessed | tf_op | source)
XLA Modules:
  0.0 80.2 jit_solution(16323086339372019871)
XLA Ops:
  1.3 0.0 copy-start.5
  1.3 0.0 copy-start.6
  1.3 0.0 copy-start.2
  1.3 0.7 copy-done.5
  2.0 0.0 copy-done.6
  2.0 0.0 copy-start.3
  2.0 0.0 copy-start.4
  2.0 0.0 copy-done.2
  2.0 0.7 copy-done.3
  2.7 0.0 copy-done.4
  2.7 0.0 copy-start
  2.7 0.9 %copy-done = bf16[256,256]{1,0:T(8,128)(2,1)S(1)} copy-done((bf16[256,256]{1,0:T(8,128)(2,1)S(1)}, bf16[256,256]{1,0:T(8,128)(2,1)}, u32[]{:S(2)}) %copy-start) | copy-done | bytes 131096
  3.6 0.0 copy-start.1
  3.6 0.8 %copy-done.1 = bf16[1,1,1,128,256]{4,3,2,1,0:T(8,128)(2,1)S(1)} copy-done((bf16[1,1,1,128,256]{4,3,2,1,0:T(8,128)(2,1)S(1)}, bf16[1,1,1,128,256]{4,3,2,1,0:T(8,128)(2,1)}, u32[]{:S(2)}) %copy-start.1) | copy-done | bytes 65560
  4.4 74.4 %message_passing.1 = (bf16[128,256]{1,0:T(8,128)(2,1)S(1)}, f32[8,128]{1,0:T(8,128)S(1)}) custom-call(s32[1]{0:T(128)} %bitcast.14.count_ref, f32[3,128]{1,0:T(4,128)S(1)} %get-tuple-element.9.offs_ref, bf16[128,256]{1,0:T(8,128)(2,1)S(1)} %bitcast.15, s32[1,128]{1,0:T(1,128)S(1)} %bitcast.17, f32[3,128]{1,0:T(4,128)S(1)} %get-tuple-element.8.targ_ref, ...), custom_call_target="tpu_custom_call" | custom-call | tf_op jit(solution)/shard_map/message_passing/pallas_call | solution.py:372
  78.8 0.6 copy.10
  79.4 0.9 %convolution_bitcast_fusion = f32[1,1,1,128,256]{4,3,2,1,0:T(8,128)} fusion(bf16[128,256]{1,0:T(8,128)(2,1)S(1)} %get-tuple-element.5, bf16[256,256]{1,0:T(8,128)(2,1)S(1)} %copy-done), kind=kOutput, calls=%fused_computation | convolution fusion | flops 16777216 | bytes 327680 | tf_op jit(solution)/shard_map/dot_general | solution.py:416
  (2 shorter events, 0.0 us)
Async XLA Ops:
  1.3 0.7 copy-start.5
  1.3 0.7 copy-start.6
  1.3 0.7 copy-start.2
  2.0 0.7 copy-start.3
  2.0 0.7 copy-start.4
  2.7 0.9 %copy-start = (bf16[256,256]{1,0:T(8,128)(2,1)S(1)}, bf16[256,256]{1,0:T(8,128)(2,1)}, u32[]{:S(2)}) copy-start(bf16[256,256]{1,0:T(8,128)(2,1)} %w_ref.1) | copy-start | bytes 393220
  3.6 0.8 %copy-start.1 = (bf16[1,1,1,128,256]{4,3,2,1,0:T(8,128)(2,1)S(1)}, bf16[1,1,1,128,256]{4,3,2,1,0:T(8,128)(2,1)}, u32[]{:S(2)}) copy-start(bf16[1,1,1,128,256]{4,3,2,1,0:T(8,128)(2,1)} %param.9) | copy-start | bytes 196612

commit v2 on v1

--- a/solution.py
+++ b/solution.py
@@ -14,6 +14,7 @@
 FAR_AWAY = 1.0e4
 MESH = pl.DeviceIdType.MESH
 ROWS = 32
+RUN_X = 4
 
 OWN, SIB, FAR = 0, 1, 2
 STEPS = (0, -1, 1)
@@ -25,10 +26,11 @@
 
 
 def kernel(
-    count_ref, offs_ref, feat_ref, mask_ref, targ_ref, w_ref, radial_ref, readout_ref,
+    count_ref, offs_in, feat_in, mask_in, targ_in, w_in, radial_in, readout_in,
     back_ref, pred_ref,
+    offs_ref, feat_ref, mask_ref, targ_ref, w_ref, radial_ref, readout_ref,
     proj, coords, rows_j, cols_i, kern_f, kern_b, msg, rhs, partial, acts, errs, zcols,
-    part_sib, got_sib, part_gz, got_gz, part_far, got_far, send_sem, recv_sem,
+    part_sib, got_sib, part_gz, got_gz, part_far, got_far, send_sem, recv_sem, load_sem,
 ):
     atoms, width = feat_ref.shape
     bases = radial_ref.shape[0]
@@ -44,6 +46,12 @@
     to_gx = {1: ((gx + nx - 1) % nx, gy, gz), 2: ((gx + 1) % nx, gy, gz)}
     to_gz = {1: (gx, gy, (gz + nz - 1) % nz), 2: (gx, gy, (gz + 1) % nz)}
     flip = {1: 2, 2: 1}
+    cross = {1: gz % RUN_X == 0, 2: gz % RUN_X == RUN_X - 1}
+    inside = {1: gz % RUN_X != 0, 2: gz % RUN_X != RUN_X - 1}
+    seam = {1: gz == 0, 2: gz == nz - 1}
+    no_seam = {1: gz != 0, 2: gz != nz - 1}
+    edge = {1: (gz % RUN_X == 0) & (gz != 0), 2: (gz % RUN_X == RUN_X - 1) & (gz != nz - 1)}
+    on_seam = {1: 1 - (gz + nz - 1) // nz, 2: (gz + 1) // nz}
     sib_step = (1 - 2 * core).astype(f32)
     role_step = (0.0, sib_step, -sib_step)
 
@@ -51,37 +59,55 @@
     for other in (far, to_gz[1], to_gz[2], to_gx[1], to_gx[2], sib):
         pl.semaphore_signal(barrier, inc=1, device_id=other, device_id_type=MESH)
 
+    loads = [
+        pltpu.make_async_copy(src, dst, load_sem.at[n])
+        for n, (src, dst) in enumerate(
+            (
+                (feat_in, feat_ref), (w_in, w_ref), (offs_in, offs_ref), (mask_in, mask_ref),
+                (targ_in, targ_ref), (radial_in, radial_ref), (readout_in, readout_ref),
+            )
+        )
+    ]
+    for load in loads:
+        load.start()
+
     copies = {}
 
-    def send(name, src, dst, device):
+    def copy_of(name, src, dst, device):
         index = len(copies)
-        copy = pltpu.make_async_remote_copy(
+        copies[name] = pltpu.make_async_remote_copy(
             src_ref=src, dst_ref=dst, send_sem=send_sem.at[index], recv_sem=recv_sem.at[index],
             device_id=device, device_id_type=MESH,
         )
-        copies[name] = copy
-        copy.start()
 
     def wait(name):
         copies[name].wait_recv()
 
-    def send_proj(a, role, c, to):
-        here = proj.at[slot(a, role, c)]
-        kind, d = to
-        if kind == "sib":
-            send(("p", a, SIB, c), here, proj.at[slot(a, SIB, c)], sib)
-        elif kind == "far":
-            send(("p", a, FAR, c), here, proj.at[slot(a, FAR, c)], far)
-        elif kind == "gz":
-            send(("p", a, role, flip[d]), here, proj.at[slot(a, role, flip[d])], to_gz[d])
-        else:
-            send(("p", flip[d], role, c), here, proj.at[slot(flip[d], role, c)], to_gx[d])
-
+    def start(name):
+        copies[name].start()
+
+    def sends(name, src, dst, device):
+        copy_of(name, src, dst, device)
+        start(name)
+
+    here = lambda a, role, c: proj.at[slot(a, role, c)]
+    copy_of(("p", 0, FAR, 0), here(0, OWN, 0), here(0, FAR, 0), far)
+    for d in (1, 2):
+        for role in (OWN, FAR):
+            copy_of(("p", 0, role, flip[d]), here(0, role, 0), here(0, role, flip[d]), to_gz[d])
+            for c in (0, 1, 2):
+                copy_of(("p", flip[d], role, c), here(0, role, c), here(flip[d], role, c), to_gx[d])
+    for a in (0, 1, 2):
+        for c in (0, 1, 2):
+            copy_of(("p", a, SIB, c), here(a, OWN, c), here(a, SIB, c), sib)
+
+    for load in loads:
+        load.wait()
     lane = lax.broadcasted_iota(jnp.int32, (1, atoms), 1)
     occ_row = lane < count_ref[0]
-    own = offs_ref[...] * (1.0 / CUT)
+    own = [offs_ref[axis] * (1.0 / CUT) for axis in range(3)]
     coords[0, 0, OWN] = jnp.concatenate(
-        [jnp.where(occ_row, own[0:1], FAR_AWAY), own[1:3], jnp.zeros((5, atoms), f32)], 0
+        [jnp.where(occ_row, own[0], FAR_AWAY), own[1], own[2], jnp.zeros((5, atoms), f32)], 0
     )
     proj[slot(0, OWN, 0)] = jnp.dot(
         feat_ref[...], w_ref[...], preferred_element_type=f32
@@ -89,14 +115,14 @@
 
     pl.semaphore_wait(barrier, 6)
 
-    send("c_far", coords.at[0, 0, OWN], coords.at[0, 0, FAR], far)
-    send_proj(0, OWN, 0, ("far", 0))
-    for d in (1, 2):
-        send_proj(0, OWN, 0, ("gz", d))
-    send("c_sib", coords.at[0, 0, OWN], coords.at[0, 0, SIB], sib)
-    send_proj(0, OWN, 0, ("sib", 0))
-    for d in (1, 2):
-        send_proj(0, OWN, 0, ("gx", d))
+    sends("c_far", coords.at[0, 0, OWN], coords.at[0, 0, FAR], far)
+    start(("p", 0, FAR, 0))
+    sends("c_sib", coords.at[0, 0, OWN], coords.at[0, 0, SIB], sib)
+    for d in (1, 2):
+        pl.when(inside[d])(lambda d=d: start(("p", 0, OWN, flip[d])))
+    for d in (1, 2):
+        start(("p", flip[d], OWN, 0))
+    start(("p", 0, SIB, 0))
 
     row_id = lax.broadcasted_iota(jnp.int32, (ROWS, atoms), 0)
     col_id = lax.broadcasted_iota(jnp.int32, (ROWS, atoms), 1)
@@ -186,62 +212,101 @@
 
         lax.fori_loop(0, count * (atoms // ROWS), one, 0)
 
+    def pass_own(c):
+        wait(("p", 0, OWN, c))
+        for d in (1, 2):
+            start(("p", flip[d], OWN, c))
+        start(("p", 0, SIB, c))
+
+    def pass_sib(c):
+        for a in (1, 2):
+            wait(("p", a, OWN, c))
+            start(("p", a, SIB, c))
+
+    def pass_far(c):
+        wait(("p", 0, FAR, c))
+        for d in (1, 2):
+            start(("p", flip[d], FAR, c))
+
     place_rows(0, OWN, 0)
     place_cols([(OWN, 0)])
     forward_slots([(slot(0, OWN, 0), 1, 1)], diag=True)
+    backward_blocks(8, 1, (0,), diag=True)
 
     wait("c_sib")
-    wait(("p", 0, SIB, 0))
-    for a in (1, 2):
-        wait(("p", a, OWN, 0))
-        send_proj(a, OWN, 0, ("sib", 0))
+    for d in (1, 2):
+        sends(("c_gz1", flip[d]), coords.at[0, 0, 0:2], coords.at[0, flip[d], 0:2], to_gz[d])
+    pass_sib(0)
+    for c in (1, 2):
+        pl.when(inside[c])(lambda c=c: pass_own(c))
+    place_rows(0, SIB, 0)
+    forward_slots([(slot(0, SIB, 0), 1, 1)])
+
     wait("c_far")
     for d in (1, 2):
-        send(("c_gz", flip[d]), coords.at[0, 0], coords.at[0, flip[d]], to_gz[d])
-    place_rows(0, SIB, 0)
-    place_rows(0, FAR, 0)
-    forward_slots([(slot(0, SIB, 0), 2, 9)])
-    for c in (1, 2):
-        wait(("p", 0, OWN, c))
-        for d in (1, 2):
-            send_proj(0, OWN, c, ("gx", d))
-        send_proj(0, OWN, c, ("sib", 0))
-    wait(("p", 0, FAR, 0))
-    for d in (1, 2):
-        send_proj(0, FAR, 0, ("gz", d))
-    for d in (1, 2):
-        send_proj(0, FAR, 0, ("gx", d))
-    for c in (1, 2):
-        wait(("c_gz", c))
-    for d in (1, 2):
-        send(("c_gx", flip[d]), coords.at[0], coords.at[flip[d]], to_gx[d])
-    for a in (1, 2):
-        for c in (1, 2):
-            wait(("p", a, OWN, c))
-            send_proj(a, OWN, c, ("sib", 0))
-    for role in (OWN, SIB, FAR):
+        sends(("c_gz2", flip[d]), coords.at[0, 0, FAR], coords.at[0, flip[d], FAR], to_gz[d])
+    for d in (1, 2):
+        pl.when(cross[d])(lambda d=d: start(("p", 0, OWN, flip[d])))
+    for c in (1, 2):
+        wait(("c_gz1", c))
+    for d in (1, 2):
+        sends(("c_gx1", flip[d]), coords.at[0, :, 0:2], coords.at[flip[d], :, 0:2], to_gx[d])
+    for c in (1, 2):
+        pl.when(inside[c])(lambda c=c: pass_sib(c))
+    for role in (OWN, SIB):
         for c in (1, 2):
             place_rows(0, role, c)
-    forward_slots([(slot(0, role, 1), 2, 1) for role in (OWN, SIB, FAR)])
-    for c in (1, 2):
-        wait(("p", 0, FAR, c))
-        for d in (1, 2):
-            send_proj(0, FAR, c, ("gx", d))
+    place_rows(0, FAR, 0)
+    forward_slots([(slot(0, role, 1), 2, 1) for role in (OWN, SIB)])
     for a in (1, 2):
-        wait(("c_gx", a))
-        for role in (OWN, SIB, FAR):
+        wait(("c_gx1", a))
+        for role in (OWN, SIB):
             for c in (0, 1, 2):
                 place_rows(a, role, c)
-    forward_slots([(slot(1, role, 0), 6, 1) for role in (OWN, SIB, FAR)])
-    place_cols(list(TARGETS))
-    backward_blocks(0, 8, (0, 1, 2))
-    backward_blocks(8, 1, (0,), diag=True)
+    forward_slots([(slot(1, role, 0), 6, 1) for role in (OWN, SIB)])
+
+    wait(("p", 0, FAR, 0))
+    for d in (1, 2):
+        start(("p", 0, FAR, flip[d]))
+    for d in (1, 2):
+        start(("p", flip[d], FAR, 0))
+    for c in (1, 2):
+        wait(("c_gz2", c))
+        place_rows(0, FAR, c)
+    for d in (1, 2):
+        sends(("c_gx2", flip[d]), coords.at[0, :, FAR], coords.at[flip[d], :, FAR], to_gx[d])
+    forward_slots([(slot(0, FAR, 0), 1, 1)])
+    place_cols([where for where in TARGETS if where != (OWN, 0)])
+    backward_blocks(2, 5, (0, 1, 2))
+    for c in (1, 2):
+        pl.when(inside[c])(lambda c=c: pass_far(c))
+
+    def cross_pass(c):
+        pass_own(c)
+        pass_far(c)
+
+    for c in (1, 2):
+        pl.when(edge[c])(lambda c=c: cross_pass(c))
+    for c in (1, 2):
+        pl.when(edge[c])(lambda c=c: pass_sib(c))
+    for a in (1, 2):
+        wait(("c_gx2", a))
+        for c in (0, 1, 2):
+            place_rows(a, FAR, c)
+    forward_slots([(slot(0, FAR, 1), 8, 1)])
+    backward_blocks(0, 2, (0, 1, 2))
+    backward_blocks(7, 1, (0, 1, 2))
     backward_blocks(8, 1, (1, 2))
+    for c in (1, 2):
+        pl.when(seam[c])(lambda c=c: pass_own(c))
+    for c in (1, 2):
+        pl.when(seam[c])(lambda c=c: pass_sib(c))
+    for c in (1, 2):
+        pl.when(seam[c])(lambda c=c: pass_far(c))
 
     for a in (0, 1, 2):
         for c in (0, 1, 2):
-            if (a, c) != (0, 0):
-                wait(("p", a, SIB, c))
+            wait(("p", a, SIB, c))
     near = 18 * atoms
     msg[...] = jnp.dot(
         kern_f[:, :, :near].reshape(kinds * atoms, near),
@@ -263,7 +328,7 @@
     readout = readout_ref[...]
     info = jnp.concatenate(
         [
-            targ_ref[...],
+            targ_ref[0], targ_ref[1], targ_ref[2],
             jnp.where(occ_row, mask_ref[...].astype(f32) * LOSS_WEIGHT, 0.0),
             jnp.zeros((atoms - 4, atoms), f32),
         ],
@@ -292,12 +357,13 @@
         acts[0, 0, at] = (pull * readout * gate * (1.0 - gate)).astype(bf16)
         acts[0, 1, at] = gates.astype(bf16)
     turned = jnp.transpose(zcols[...])
-    pred_ref[...] = turned[0:8]
+    for c in range(3):
+        pred_ref[c] = turned[c : c + 1]
     errs[0] = turned[0:8]
 
     for d in (1, 2):
-        send(("act", flip[d]), acts.at[0], acts.at[flip[d]], to_gx[d])
-        send(("err", flip[d]), errs.at[0], errs.at[flip[d]], to_gx[d])
+        sends(("act", flip[d]), acts.at[0], acts.at[flip[d]], to_gx[d])
+        sends(("err", flip[d]), errs.at[0], errs.at[flip[d]], to_gx[d])
 
     def build_rhs(a, cols, first):
         for q in range(atoms // ROWS):
@@ -335,32 +401,39 @@
 
     part_gz[1] = totals(0, 2).astype(bf16)
     for d in (1, 2):
-        send(("far_gz", flip[d]), part_gz.at[1, d - 1], got_gz.at[1, flip[d] - 1], to_gz[d])
+        gx_d, gy_d, gz_d = to_gz[d]
+        device = (gx_d, gy_d + on_seam[d] * (far_gy - gy_d), gz_d)
+        sends(("far_gz", flip[d]), part_gz.at[1, d - 1], got_gz.at[1, flip[d] - 1], device)
+    partial[7] = totals(7, 1)[0]
     part_sib[...] = totals(2, 3).astype(bf16)
-    send("sib", part_sib, got_sib, sib)
+    sends("sib", part_sib, got_sib, sib)
+
+    def add_far_gz(c, n):
+        wait(("far_gz", c))
+        partial[n] = partial[n] + got_gz[1, c - 1].astype(f32)
+
+    for c in (1, 2):
+        pl.when(no_seam[c])(lambda c=c: add_far_gz(c, 7))
+    part_far[...] = partial[7].astype(bf16)
+    sends("far", part_far, got_far, far)
     partial[5:7] = totals(5, 2)
     wait("sib")
     part_gz[0] = (partial[5:7] + got_sib[0:2].astype(f32)).astype(bf16)
     for d in (1, 2):
-        send(("own_gz", flip[d]), part_gz.at[0, d - 1], got_gz.at[0, flip[d] - 1], to_gz[d])
-    partial[7:9] = totals(7, 2)
-    for c in (1, 2):
-        wait(("far_gz", c))
-    part_far[...] = (
-        partial[7] + got_gz[1, 0].astype(f32) + got_gz[1, 1].astype(f32)
-    ).astype(bf16)
-    send("far", part_far, got_far, far)
+        sends(("own_gz", flip[d]), part_gz.at[0, d - 1], got_gz.at[0, flip[d] - 1], to_gz[d])
+    partial[8] = totals(8, 1)[0] + got_sib[2].astype(f32)
     for c in (1, 2):
         wait(("own_gz", c))
-    total = partial[8] + got_sib[2].astype(f32)
-    total = total + got_gz[0, 0].astype(f32) + got_gz[0, 1].astype(f32)
+    partial[8] = partial[8] + got_gz[0, 0].astype(f32) + got_gz[0, 1].astype(f32)
+    for c in (1, 2):
+        pl.when(seam[c])(lambda c=c: add_far_gz(c, 8))
     wait("far")
-    back_ref[...] = (total + got_far[...].astype(f32)).astype(bf16)
+    back_ref[...] = (partial[8] + got_far[...].astype(f32)).astype(bf16)
     for copy in copies.values():
         copy.wait_send()
 
 
-COPIES = 26 + 6 + 4 + 6
+COPIES = 26 + 10 + 4 + 6
 
 
 def on_device(offsets, features, counts, mask, targets, w_in, radial, readout):
@@ -373,11 +446,18 @@
         kernel,
         out_shape=(
             jax.ShapeDtypeStruct((atoms, width), bf16),
-            jax.ShapeDtypeStruct((8, atoms), f32),
+            jax.ShapeDtypeStruct((3, 1, atoms), f32),
         ),
-        in_specs=[pl.BlockSpec(memory_space=pltpu.SMEM)] + [vmem] * 7,
+        in_specs=[pl.BlockSpec(memory_space=pltpu.SMEM)] + [pl.BlockSpec(memory_space=pl.ANY)] * 7,
         out_specs=(vmem, vmem),
         scratch_shapes=[
+            pltpu.VMEM((3, 1, atoms), f32),
+            pltpu.VMEM((atoms, width), bf16),
+            pltpu.VMEM((1, atoms), jnp.int32),
+            pltpu.VMEM((3, 1, atoms), f32),
+            pltpu.VMEM(w_in.shape, bf16),
+            pltpu.VMEM(radial.shape, f32),
+            pltpu.VMEM((1, width), f32),
             pltpu.VMEM((27, atoms, width), bf16),
             pltpu.VMEM((3, 3, 3, 8, atoms), f32),
             pltpu.VMEM((27, 8, atoms), f32),
@@ -398,17 +478,18 @@
             pltpu.VMEM((atoms, width), bf16),
             pltpu.SemaphoreType.DMA((COPIES,)),
             pltpu.SemaphoreType.DMA((COPIES,)),
+            pltpu.SemaphoreType.DMA((7,)),
         ],
         compiler_params=pltpu.CompilerParams(
-            collective_id=0, has_side_effects=True, vmem_limit_bytes=48 << 20
+            collective_id=0, has_side_effects=True, vmem_limit_bytes=60 << 20
         ),
         name="message_passing",
     )(
         counts.reshape(1),
-        offsets.reshape(3, atoms),
+        offsets.reshape(3, 1, atoms),
         features.reshape(atoms, width),
         mask.reshape(1, atoms),
-        targets.reshape(3, atoms),
+        targets.reshape(3, 1, atoms),
         w_in,
         radial,
         readout.reshape(1, width),
@@ -416,7 +497,7 @@
     grad = lax.dot_general(
         back, w_in, (((1,), (1,)), ((), ())), preferred_element_type=jnp.float32
     )
-    return (pred[0:3].reshape(1, 1, 1, 3, atoms), grad.reshape(1, 1, 1, atoms, width))
+    return (pred.reshape(1, 1, 1, 3, atoms), grad.reshape(1, 1, 1, atoms, width))
 
 
 def solution(mesh):

time: 80.5 us -> 80.7 us (level)
  local copies, waits for them, and re-layouts: 3.67 us -> 0.57 us
  Pallas kernels: 74.4 us -> 76.8 us
  matrix products: 0.86 us -> 1.7 us
    unnamed x16 -> x5, local copies, waits for them, and re-layouts: 3.66 us -> 0.57 us
    pallas_call x1, Pallas kernels: 74.4 us -> 76.8 us  [on_device(): pl.pallas_call(kernel, out_shape=(jax.ShapeDtypeStruct((atoms, width), bf...]
    dot_general x1, matrix products: 0.86 us -> 1.7 us  [on_device(): lax.dot_general(back, w_in, (((1,), (1,)), ((), ())), preferred_element_t...]
where the time goes in v2:
time: 80.7 us; the launch traced here: 80.4 us
  Pallas kernels  76.8 us (95%)
  matrix products  1.7 us (2%)
  between operations  1.35 us (2%)
    pallas_call x1, Pallas kernels, on_device(): pl.pallas_call(kernel, out_shape=(jax.ShapeDtypeStruct((atoms, width), bf...  76.8 us
    dot_general x1, matrix products, on_device(): lax.dot_general(back, w_in, (((1,), (1,)), ((), ())), preferred_element_t...  1.7 us

profile of v2, /device:TPU:1, one launch (start us, length us, event | category | flops | bytes accessed | tf_op | source)
XLA Modules:
  0.0 80.4 jit_solution(11881380654845991493)
XLA Ops:
  0.6 0.0 copy-start
  1.3 76.8 %message_passing.1 = (bf16[128,256]{1,0:T(8,128)(2,1)}, f32[3,1,128]{2,1,0:T(1,128)}) custom-call(s32[1]{0:T(128)} %bitcast.13.count_ref, f32[3,1,128]{2,1,0:T(1,128)} %bitcast.15, bf16[128,256]{1,0:T(8,128)(2,1)} %bitcast.14, s32[1,128]{1,0:T(1,128)} %bitcast.19, f32[3,1,128]{2,1,0:T(1,128)} %bitcast.16, bf16[256,256]{1,0:T(8,128)(2,1)} %w_in.1, ...), custom_call_target="tpu_custom_call" | custom-call | tf_op jit(solution)/shard_map/message_passing/pallas_call | solution.py:445
  78.2 0.0 copy-done
  78.2 0.0 copy-start.1
  78.2 1.7 %convolution_bitcast_fusion = f32[1,1,1,128,256]{4,3,2,1,0:T(8,128)} fusion(bf16[128,256]{1,0:T(8,128)(2,1)} %get-tuple-element.5, bf16[256,256]{1,0:T(8,128)(2,1)S(1)} %copy-done), kind=kOutput, calls=%fused_computation | convolution fusion | flops 16777216 | bytes 327680 | tf_op jit(solution)/shard_map/dot_general | solution.py:497
  79.9 0.0 copy-done.1
  79.9 0.6 copy.13
Async XLA Ops:
  0.6 77.5 %copy-start = (bf16[256,256]{1,0:T(8,128)(2,1)S(1)}, bf16[256,256]{1,0:T(8,128)(2,1)}, u32[]{:S(2)}) copy-start(bf16[256,256]{1,0:T(8,128)(2,1)} %w_in.1) | copy-start | bytes 393220
  78.2 1.7 %copy-start.1 = (f32[3,1,128]{2,1,0:T(1,128)S(1)}, f32[3,1,128]{2,1,0:T(1,128)}, u32[]{:S(2)}) copy-start(f32[3,1,128]{2,1,0:T(1,128)} %get-tuple-element.4) | copy-start | bytes 4612

commit v3 on v2

--- a/solution.py
+++ b/solution.py
@@ -22,7 +22,7 @@
 
 
 def slot(a, role, c):
-    return role * 9 + a * 3 + c
+    return 18 + c * 3 + a if role == FAR else c * 6 + a * 2 + role
 
 
 def kernel(
@@ -228,6 +228,31 @@
         for d in (1, 2):
             start(("p", flip[d], FAR, c))
 
+    def gather(first, count):
+        lo, hi = first * atoms, (first + count) * atoms
+        return jnp.dot(
+            kern_f[:, :, lo:hi].reshape(kinds * atoms, hi - lo),
+            proj[first : first + count].reshape(hi - lo, width),
+            preferred_element_type=f32,
+        ).reshape(kinds, atoms, width)
+
+    def near_sum(c):
+        for a in (0, 1, 2):
+            wait(("p", a, SIB, c))
+        msg[...] = gather(6 * c, 6) if c == 0 else msg[...] + gather(6 * c, 6)
+
+    def far_sum(c):
+        for a in (1, 2):
+            wait(("p", a, FAR, c))
+        msg[...] = msg[...] + gather(18 + 3 * c, 3)
+
+    def take_far():
+        wait(("p", 0, FAR, 0))
+        for d in (1, 2):
+            start(("p", 0, FAR, flip[d]))
+        for d in (1, 2):
+            start(("p", flip[d], FAR, 0))
+
     place_rows(0, OWN, 0)
     place_cols([(OWN, 0)])
     forward_slots([(slot(0, OWN, 0), 1, 1)], diag=True)
@@ -241,86 +266,116 @@
         pl.when(inside[c])(lambda c=c: pass_own(c))
     place_rows(0, SIB, 0)
     forward_slots([(slot(0, SIB, 0), 1, 1)])
-
-    wait("c_far")
-    for d in (1, 2):
-        sends(("c_gz2", flip[d]), coords.at[0, 0, FAR], coords.at[0, flip[d], FAR], to_gz[d])
-    for d in (1, 2):
-        pl.when(cross[d])(lambda d=d: start(("p", 0, OWN, flip[d])))
+    for d in (1, 2):
+        copy_of(("c_gz2", flip[d]), coords.at[0, 0, FAR], coords.at[0, flip[d], FAR], to_gz[d])
+        copy_of(
+            ("c_gx1", flip[d]), coords.at[0, :, 0:2], coords.at[flip[d], :, 0:2], to_gx[d]
+        )
+        copy_of(("c_gx2", flip[d]), coords.at[0, :, FAR], coords.at[flip[d], :, FAR], to_gx[d])
+
+    def coords_far():
+        wait("c_far")
+        for d in (1, 2):
+            start(("c_gz2", flip[d]))
+        for d in (1, 2):
+            pl.when(cross[d])(lambda d=d: start(("p", 0, OWN, flip[d])))
+
+    def coords_gz1():
+        for c in (1, 2):
+            wait(("c_gz1", c))
+        for d in (1, 2):
+            start(("c_gx1", flip[d]))
+        for role in (OWN, SIB):
+            for c in (1, 2):
+                place_rows(0, role, c)
+        forward_slots([(slot(0, OWN, c), 2, 1) for c in (1, 2)])
+
+    def coords_gx1():
+        for a in (1, 2):
+            wait(("c_gx1", a))
+            for role in (OWN, SIB):
+                for c in (0, 1, 2):
+                    place_rows(a, role, c)
+        forward_slots([(slot(1, OWN, c), 4, 1) for c in (0, 1, 2)])
+
+    def coords_gz2():
+        for c in (1, 2):
+            wait(("c_gz2", c))
+        for d in (1, 2):
+            start(("c_gx2", flip[d]))
+        for c in (0, 1, 2):
+            place_rows(0, FAR, c)
+        forward_slots([(slot(0, FAR, 0), 1, 1)])
+
+    def coords_gx2():
+        for a in (1, 2):
+            wait(("c_gx2", a))
+            for c in (0, 1, 2):
+                place_rows(a, FAR, c)
+        forward_slots([(slot(1, FAR, 0), 8, 1)])
+
+    def backward_near():
+        place_cols([where for where in TARGETS if where != (OWN, 0)])
+        backward_blocks(2, 5, (0, 1, 2))
+        backward_blocks(8, 1, (1, 2))
+
+    def backward_far():
+        backward_blocks(0, 2, (0, 1, 2))
+        backward_blocks(7, 1, (0, 1, 2))
+
+    def plain():
+        coords_gz1()
+        for c in (1, 2):
+            pl.when(inside[c])(lambda c=c: pass_sib(c))
+        coords_far()
+        coords_gx1()
+        near_sum(0)
+        for c in (1, 2):
+            pl.when(inside[c])(lambda c=c: near_sum(c))
+        for c in (1, 2):
+            pl.when(cross[c])(lambda c=c: pass_own(c))
+        take_far()
+        coords_gz2()
+        backward_near()
+        for c in (1, 2):
+            pl.when(inside[c])(lambda c=c: pass_far(c))
+        for c in (1, 2):
+            pl.when(cross[c])(lambda c=c: pass_sib(c))
+        for c in (1, 2):
+            pl.when(cross[c])(lambda c=c: pass_far(c))
+        coords_gx2()
+        backward_far()
+        for c in (1, 2):
+            pl.when(cross[c])(lambda c=c: near_sum(c))
+        far_sum(0)
+        for c in (1, 2):
+            pl.when(inside[c])(lambda c=c: far_sum(c))
+        for c in (1, 2):
+            pl.when(cross[c])(lambda c=c: far_sum(c))
+
+    def at_seam(c):
+        other = flip[c]
+        coords_far()
+        pass_sib(other)
+        coords_gz1()
+        take_far()
+        coords_gx1()
+        near_sum(0)
+        coords_gz2()
+        pass_own(c)
+        near_sum(other)
+        pass_far(other)
+        coords_gx2()
+        pass_sib(c)
+        far_sum(0)
+        pass_far(c)
+        near_sum(c)
+        far_sum(other)
+        far_sum(c)
+
+    pl.when((gz != 0) & (gz != nz - 1))(plain)
     for c in (1, 2):
-        wait(("c_gz1", c))
-    for d in (1, 2):
-        sends(("c_gx1", flip[d]), coords.at[0, :, 0:2], coords.at[flip[d], :, 0:2], to_gx[d])
-    for c in (1, 2):
-        pl.when(inside[c])(lambda c=c: pass_sib(c))
-    for role in (OWN, SIB):
-        for c in (1, 2):
-            place_rows(0, role, c)
-    place_rows(0, FAR, 0)
-    forward_slots([(slot(0, role, 1), 2, 1) for role in (OWN, SIB)])
-    for a in (1, 2):
-        wait(("c_gx1", a))
-        for role in (OWN, SIB):
-            for c in (0, 1, 2):
-                place_rows(a, role, c)
-    forward_slots([(slot(1, role, 0), 6, 1) for role in (OWN, SIB)])
-
-    wait(("p", 0, FAR, 0))
-    for d in (1, 2):
-        start(("p", 0, FAR, flip[d]))
-    for d in (1, 2):
-        start(("p", flip[d], FAR, 0))
-    for c in (1, 2):
-        wait(("c_gz2", c))
-        place_rows(0, FAR, c)
-    for d in (1, 2):
-        sends(("c_gx2", flip[d]), coords.at[0, :, FAR], coords.at[flip[d], :, FAR], to_gx[d])
-    forward_slots([(slot(0, FAR, 0), 1, 1)])
-    place_cols([where for where in TARGETS if where != (OWN, 0)])
-    backward_blocks(2, 5, (0, 1, 2))
-    for c in (1, 2):
-        pl.when(inside[c])(lambda c=c: pass_far(c))
-
-    def cross_pass(c):
-        pass_own(c)
-        pass_far(c)
-
-    for c in (1, 2):
-        pl.when(edge[c])(lambda c=c: cross_pass(c))
-    for c in (1, 2):
-        pl.when(edge[c])(lambda c=c: pass_sib(c))
-    for a in (1, 2):
-        wait(("c_gx2", a))
-        for c in (0, 1, 2):
-            place_rows(a, FAR, c)
-    forward_slots([(slot(0, FAR, 1), 8, 1)])
-    backward_blocks(0, 2, (0, 1, 2))
-    backward_blocks(7, 1, (0, 1, 2))
-    backward_blocks(8, 1, (1, 2))
-    for c in (1, 2):
-        pl.when(seam[c])(lambda c=c: pass_own(c))
-    for c in (1, 2):
-        pl.when(seam[c])(lambda c=c: pass_sib(c))
-    for c in (1, 2):
-        pl.when(seam[c])(lambda c=c: pass_far(c))
-
-    for a in (0, 1, 2):
-        for c in (0, 1, 2):
-            wait(("p", a, SIB, c))
-    near = 18 * atoms
-    msg[...] = jnp.dot(
-        kern_f[:, :, :near].reshape(kinds * atoms, near),
-        proj[0:18].reshape(near, width),
-        preferred_element_type=f32,
-    ).reshape(kinds, atoms, width)
-    for a in (1, 2):
-        for c in (0, 1, 2):
-            wait(("p", a, FAR, c))
-    msg[...] = msg[...] + jnp.dot(
-        kern_f[:, :, near:].reshape(kinds * atoms, 9 * atoms),
-        proj[18:27].reshape(9 * atoms, width),
-        preferred_element_type=f32,
-    ).reshape(kinds, atoms, width)
+        pl.when(seam[c])(lambda c=c: at_seam(c))
 
     weights = [
         radial_ref[b : b + 1] * math.exp(-GAMMA * (b / (bases - 1)) ** 2) for b in range(bases)
@@ -376,8 +431,13 @@
                 err = cols[q * ROWS : (q + 1) * ROWS, first + c : first + c + 1]
                 rhs[a * kinds + bases + c, at] = (gates * (-err)).astype(bf16)
 
+    def late_backward():
+        backward_near()
+        backward_far()
+
     build_rhs(0, zcols[...], 3)
     part = kinds * atoms
+    pl.when((gz == 0) | (gz == nz - 1))(late_backward)
     partial[...] = jnp.dot(
         kern_b[:, :, :part].reshape(9 * atoms, part),
         rhs[0:kinds].reshape(part, width),
@@ -404,9 +464,14 @@
         gx_d, gy_d, gz_d = to_gz[d]
         device = (gx_d, gy_d + on_seam[d] * (far_gy - gy_d), gz_d)
         sends(("far_gz", flip[d]), part_gz.at[1, d - 1], got_gz.at[1, flip[d] - 1], device)
-    partial[7] = totals(7, 1)[0]
     part_sib[...] = totals(2, 3).astype(bf16)
     sends("sib", part_sib, got_sib, sib)
+    partial[5:7] = totals(5, 2)
+    partial[7] = totals(7, 1)[0]
+    wait("sib")
+    part_gz[0] = (partial[5:7] + got_sib[0:2].astype(f32)).astype(bf16)
+    for d in (1, 2):
+        sends(("own_gz", flip[d]), part_gz.at[0, d - 1], got_gz.at[0, flip[d] - 1], to_gz[d])
 
     def add_far_gz(c, n):
         wait(("far_gz", c))
@@ -416,11 +481,6 @@
         pl.when(no_seam[c])(lambda c=c: add_far_gz(c, 7))
     part_far[...] = partial[7].astype(bf16)
     sends("far", part_far, got_far, far)
-    partial[5:7] = totals(5, 2)
-    wait("sib")
-    part_gz[0] = (partial[5:7] + got_sib[0:2].astype(f32)).astype(bf16)
-    for d in (1, 2):
-        sends(("own_gz", flip[d]), part_gz.at[0, d - 1], got_gz.at[0, flip[d] - 1], to_gz[d])
     partial[8] = totals(8, 1)[0] + got_sib[2].astype(f32)
     for c in (1, 2):
         wait(("own_gz", c))

time: 80.7 us -> 76.3 us (0.945)
  Pallas kernels: 76.8 us -> 72.4 us
    pallas_call x1, Pallas kernels: 76.8 us -> 72.4 us  [on_device(): pl.pallas_call(kernel, out_shape=(jax.ShapeDtypeStruct((atoms, width), bf...]
where the time goes in v3:
time: 76.3 us; the launch traced here: 76 us
  Pallas kernels  72.4 us (95%)
  matrix products  1.69 us (2%)
  between operations  1.35 us (2%)
    pallas_call x1, Pallas kernels, on_device(): pl.pallas_call(kernel, out_shape=(jax.ShapeDtypeStruct((atoms, width), bf...  72.4 us
    dot_general x1, matrix products, on_device(): lax.dot_general(back, w_in, (((1,), (1,)), ((), ())), preferred_element_t...  1.69 us

profile of v3, /device:TPU:1, one launch (start us, length us, event | category | flops | bytes accessed | tf_op | source)
XLA Modules:
  0.0 76.0 jit_solution(8009767737489268027)
XLA Ops:
  0.6 0.0 copy-start
  1.3 72.4 %message_passing.1 = (bf16[128,256]{1,0:T(8,128)(2,1)}, f32[3,1,128]{2,1,0:T(1,128)}) custom-call(s32[1]{0:T(128)} %bitcast.13.count_ref, f32[3,1,128]{2,1,0:T(1,128)} %bitcast.15, bf16[128,256]{1,0:T(8,128)(2,1)} %bitcast.14, s32[1,128]{1,0:T(1,128)} %bitcast.19, f32[3,1,128]{2,1,0:T(1,128)} %bitcast.16, bf16[256,256]{1,0:T(8,128)(2,1)} %w_in.1, ...), custom_call_target="tpu_custom_call" | custom-call | tf_op jit(solution)/shard_map/message_passing/pallas_call | solution.py:505
  73.8 0.0 copy-done
  73.8 0.0 copy-start.1
  73.8 1.7 %convolution_bitcast_fusion = f32[1,1,1,128,256]{4,3,2,1,0:T(8,128)} fusion(bf16[128,256]{1,0:T(8,128)(2,1)} %get-tuple-element.5, bf16[256,256]{1,0:T(8,128)(2,1)S(1)} %copy-done), kind=kOutput, calls=%fused_computation | convolution fusion | flops 16777216 | bytes 327680 | tf_op jit(solution)/shard_map/dot_general | solution.py:557
  75.5 0.0 copy-done.1
  75.5 0.6 copy.13
Async XLA Ops:
  0.6 73.1 %copy-start = (bf16[256,256]{1,0:T(8,128)(2,1)S(1)}, bf16[256,256]{1,0:T(8,128)(2,1)}, u32[]{:S(2)}) copy-start(bf16[256,256]{1,0:T(8,128)(2,1)} %w_in.1) | copy-start | bytes 393220
  73.8 1.7 %copy-start.1 = (f32[3,1,128]{2,1,0:T(1,128)S(1)}, f32[3,1,128]{2,1,0:T(1,128)}, u32[]{:S(2)}) copy-start(f32[3,1,128]{2,1,0:T(1,128)} %get-tuple-element.4) | copy-start | bytes 4612

commit v4 on v3

--- a/solution.py
+++ b/solution.py
@@ -30,7 +30,8 @@
     back_ref, pred_ref,
     offs_ref, feat_ref, mask_ref, targ_ref, w_ref, radial_ref, readout_ref,
     proj, coords, rows_j, cols_i, kern_f, kern_b, msg, rhs, partial, acts, errs, zcols,
-    part_sib, got_sib, part_gz, got_gz, part_far, got_far, send_sem, recv_sem, load_sem,
+    part_sib, got_sib, part_gz, got_gz, part_far, got_far, part_seam, got_seam,
+    send_sem, recv_sem, load_sem,
 ):
     atoms, width = feat_ref.shape
     bases = radial_ref.shape[0]
@@ -51,7 +52,6 @@
     seam = {1: gz == 0, 2: gz == nz - 1}
     no_seam = {1: gz != 0, 2: gz != nz - 1}
     edge = {1: (gz % RUN_X == 0) & (gz != 0), 2: (gz % RUN_X == RUN_X - 1) & (gz != nz - 1)}
-    on_seam = {1: 1 - (gz + nz - 1) // nz, 2: (gz + 1) // nz}
     sib_step = (1 - 2 * core).astype(f32)
     role_step = (0.0, sib_step, -sib_step)
 
@@ -91,12 +91,19 @@
         start(name)
 
     here = lambda a, role, c: proj.at[slot(a, role, c)]
-    copy_of(("p", 0, FAR, 0), here(0, OWN, 0), here(0, FAR, 0), far)
-    for d in (1, 2):
-        for role in (OWN, FAR):
-            copy_of(("p", 0, role, flip[d]), here(0, role, 0), here(0, role, flip[d]), to_gz[d])
-            for c in (0, 1, 2):
-                copy_of(("p", flip[d], role, c), here(0, role, c), here(flip[d], role, c), to_gx[d])
+    half = atoms // 2
+    part_of = lambda a, role, c, h: proj.at[slot(a, role, c), h * half : (h + 1) * half]
+    for h in (0, 1):
+        copy_of(("f", 0, 0, h), part_of(0, OWN, 0, h), part_of(0, FAR, 0, h), far)
+    for d in (1, 2):
+        e = flip[d]
+        copy_of(("p", 0, OWN, e), here(0, OWN, 0), here(0, OWN, e), to_gz[d])
+        for h in (0, 1):
+            copy_of(("f", 0, e, h), part_of(0, FAR, 0, h), part_of(0, FAR, e, h), to_gz[d])
+        for c in (0, 1, 2):
+            copy_of(("p", e, OWN, c), here(0, OWN, c), here(e, OWN, c), to_gx[d])
+            for h in (0, 1):
+                copy_of(("f", e, c, h), part_of(0, FAR, c, h), part_of(e, FAR, c, h), to_gx[d])
     for a in (0, 1, 2):
         for c in (0, 1, 2):
             copy_of(("p", a, SIB, c), here(a, OWN, c), here(a, SIB, c), sib)
@@ -116,7 +123,8 @@
     pl.semaphore_wait(barrier, 6)
 
     sends("c_far", coords.at[0, 0, OWN], coords.at[0, 0, FAR], far)
-    start(("p", 0, FAR, 0))
+    for h in (0, 1):
+        start(("f", 0, 0, h))
     sends("c_sib", coords.at[0, 0, OWN], coords.at[0, 0, SIB], sib)
     for d in (1, 2):
         pl.when(inside[d])(lambda d=d: start(("p", 0, OWN, flip[d])))
@@ -224,9 +232,10 @@
             start(("p", a, SIB, c))
 
     def pass_far(c):
-        wait(("p", 0, FAR, c))
-        for d in (1, 2):
-            start(("p", flip[d], FAR, c))
+        for h in (0, 1):
+            wait(("f", 0, c, h))
+            for d in (1, 2):
+                start(("f", flip[d], c, h))
 
     def gather(first, count):
         lo, hi = first * atoms, (first + count) * atoms
@@ -243,15 +252,17 @@
 
     def far_sum(c):
         for a in (1, 2):
-            wait(("p", a, FAR, c))
+            for h in (0, 1):
+                wait(("f", a, c, h))
         msg[...] = msg[...] + gather(18 + 3 * c, 3)
 
     def take_far():
-        wait(("p", 0, FAR, 0))
-        for d in (1, 2):
-            start(("p", 0, FAR, flip[d]))
-        for d in (1, 2):
-            start(("p", flip[d], FAR, 0))
+        for h in (0, 1):
+            wait(("f", 0, 0, h))
+            for d in (1, 2):
+                start(("f", 0, flip[d], h))
+            for d in (1, 2):
+                start(("f", flip[d], 0, h))
 
     place_rows(0, OWN, 0)
     place_cols([(OWN, 0)])
@@ -367,8 +378,8 @@
         pass_far(other)
         coords_gx2()
         pass_sib(c)
+        pass_far(c)
         far_sum(0)
-        pass_far(c)
         near_sum(c)
         far_sum(other)
         far_sum(c)
@@ -437,6 +448,7 @@
 
     build_rhs(0, zcols[...], 3)
     part = kinds * atoms
+    copy_of("seam", part_seam, got_seam, (gx, far_gy, nz - 1 - gz))
     pl.when((gz == 0) | (gz == nz - 1))(late_backward)
     partial[...] = jnp.dot(
         kern_b[:, :, :part].reshape(9 * atoms, part),
@@ -459,41 +471,72 @@
             preferred_element_type=f32,
         ).reshape(count, atoms, width)
 
-    part_gz[1] = totals(0, 2).astype(bf16)
-    for d in (1, 2):
-        gx_d, gy_d, gz_d = to_gz[d]
-        device = (gx_d, gy_d + on_seam[d] * (far_gy - gy_d), gz_d)
-        sends(("far_gz", flip[d]), part_gz.at[1, d - 1], got_gz.at[1, flip[d] - 1], device)
+    for d in (1, 2):
+        copy_of(("far_gz", flip[d]), part_gz.at[1, d - 1], got_gz.at[1, flip[d] - 1], to_gz[d])
+        copy_of(("own_gz", flip[d]), part_gz.at[0, d - 1], got_gz.at[0, flip[d] - 1], to_gz[d])
+    copy_of("far", part_far, got_far, far)
+
+    def send_far(steps):
+        total = partial[7]
+        for c in steps:
+            wait(("far_gz", c))
+            total = total + got_gz[1, c - 1].astype(f32)
+        part_far[...] = total.astype(bf16)
+        start("far")
+
+    def seam_first(c):
+        other = flip[c]
+        part_gz[1, other - 1] = totals(other - 1, 1)[0].astype(bf16)
+        start(("far_gz", c))
+        part_seam[...] = totals(c - 1, 1)[0].astype(bf16)
+        start("seam")
+        partial[7] = totals(7, 1)[0]
+        send_far((other,))
+
+    def plain_first():
+        part_gz[1] = totals(0, 2).astype(bf16)
+        for c in (1, 2):
+            start(("far_gz", c))
+
+    def plain_far():
+        partial[7] = totals(7, 1)[0]
+        send_far((1, 2))
+
+    no_seams = (gz != 0) & (gz != nz - 1)
+    for c in (1, 2):
+        pl.when(seam[c])(lambda c=c: seam_first(c))
+    pl.when(no_seams)(plain_first)
     part_sib[...] = totals(2, 3).astype(bf16)
     sends("sib", part_sib, got_sib, sib)
+    pl.when(no_seams)(plain_far)
     partial[5:7] = totals(5, 2)
-    partial[7] = totals(7, 1)[0]
     wait("sib")
     part_gz[0] = (partial[5:7] + got_sib[0:2].astype(f32)).astype(bf16)
     for d in (1, 2):
-        sends(("own_gz", flip[d]), part_gz.at[0, d - 1], got_gz.at[0, flip[d] - 1], to_gz[d])
-
-    def add_far_gz(c, n):
-        wait(("far_gz", c))
-        partial[n] = partial[n] + got_gz[1, c - 1].astype(f32)
-
-    for c in (1, 2):
-        pl.when(no_seam[c])(lambda c=c: add_far_gz(c, 7))
-    part_far[...] = partial[7].astype(bf16)
-    sends("far", part_far, got_far, far)
+        start(("own_gz", flip[d]))
     partial[8] = totals(8, 1)[0] + got_sib[2].astype(f32)
+
     for c in (1, 2):
         wait(("own_gz", c))
     partial[8] = partial[8] + got_gz[0, 0].astype(f32) + got_gz[0, 1].astype(f32)
-    for c in (1, 2):
-        pl.when(seam[c])(lambda c=c: add_far_gz(c, 8))
+
+    def add_seam():
+        wait("seam")
+        partial[8] = partial[8] + got_seam[...].astype(f32)
+
+    pl.when((gz == 0) | (gz == nz - 1))(add_seam)
     wait("far")
     back_ref[...] = (partial[8] + got_far[...].astype(f32)).astype(bf16)
-    for copy in copies.values():
-        copy.wait_send()
-
-
-COPIES = 26 + 10 + 4 + 6
+    for name, copy in copies.items():
+        if name == "seam":
+            pl.when((gz == 0) | (gz == nz - 1))(copy.wait_send)
+        elif name[0] == "far_gz":
+            pl.when(no_seam[flip[name[1]]])(copy.wait_send)
+        else:
+            copy.wait_send()
+
+
+COPIES = 26 + 9 + 10 + 4 + 6 + 1
 
 
 def on_device(offsets, features, counts, mask, targets, w_in, radial, readout):
@@ -536,6 +579,8 @@
             pltpu.VMEM((2, 2, atoms, width), bf16),
             pltpu.VMEM((atoms, width), bf16),
             pltpu.VMEM((atoms, width), bf16),
+            pltpu.VMEM((atoms, width), bf16),
+            pltpu.VMEM((atoms, width), bf16),
             pltpu.SemaphoreType.DMA((COPIES,)),
             pltpu.SemaphoreType.DMA((COPIES,)),
             pltpu.SemaphoreType.DMA((7,)),

time: 76.3 us -> 76.1 us (level)
  the two profiles are of different devices: /device:TPU:1 before, /device:TPU:3 now
where the time goes in v4:
time: 76.1 us; the launch traced here: 75.9 us
  Pallas kernels  72.3 us (95%)
  matrix products  1.7 us (2%)
  between operations  1.35 us (2%)
    pallas_call x1, Pallas kernels, on_device(): pl.pallas_call(kernel, out_shape=(jax.ShapeDtypeStruct((atoms, width), bf...  72.3 us
    dot_general x1, matrix products, on_device(): lax.dot_general(back, w_in, (((1,), (1,)), ((), ())), preferred_element_t...  1.7 us

profile of v4, /device:TPU:3, one launch (start us, length us, event | category | flops | bytes accessed | tf_op | source)
XLA Modules:
  0.0 75.9 jit_solution(2050896807820057979)
XLA Ops:
  0.6 0.0 copy-start
  1.3 72.3 %message_passing.1 = (bf16[128,256]{1,0:T(8,128)(2,1)}, f32[3,1,128]{2,1,0:T(1,128)}) custom-call(s32[1]{0:T(128)} %bitcast.13.count_ref, f32[3,1,128]{2,1,0:T(1,128)} %bitcast.15, bf16[128,256]{1,0:T(8,128)(2,1)} %bitcast.14, s32[1,128]{1,0:T(1,128)} %bitcast.19, f32[3,1,128]{2,1,0:T(1,128)} %bitcast.16, bf16[256,256]{1,0:T(8,128)(2,1)} %w_in.1, ...), custom_call_target="tpu_custom_call" | custom-call | tf_op jit(solution)/shard_map/message_passing/pallas_call | solution.py:548
  73.7 0.0 copy-done
  73.7 0.0 copy-start.1
  73.7 1.7 %convolution_bitcast_fusion = f32[1,1,1,128,256]{4,3,2,1,0:T(8,128)} fusion(bf16[128,256]{1,0:T(8,128)(2,1)} %get-tuple-element.5, bf16[256,256]{1,0:T(8,128)(2,1)S(1)} %copy-done), kind=kOutput, calls=%fused_computation | convolution fusion | flops 16777216 | bytes 327680 | tf_op jit(solution)/shard_map/dot_general | solution.py:602
  75.4 0.0 copy-done.1
  75.4 0.6 copy.13
Async XLA Ops:
  0.6 73.0 %copy-start = (bf16[256,256]{1,0:T(8,128)(2,1)S(1)}, bf16[256,256]{1,0:T(8,128)(2,1)}, u32[]{:S(2)}) copy-start(bf16[256,256]{1,0:T(8,128)(2,1)} %w_in.1) | copy-start | bytes 393220
  73.7 1.7 %copy-start.1 = (f32[3,1,128]{2,1,0:T(1,128)S(1)}, f32[3,1,128]{2,1,0:T(1,128)}, u32[]{:S(2)}) copy-start(f32[3,1,128]{2,1,0:T(1,128)} %get-tuple-element.4) | copy-start | bytes 4612
